TPU v7x, 32 devices: a whole 2x2x4 slice. The times are simulated.
32 devices in a mesh: dp: 8 (over y, x, core), mp: 4 (over z).
Axes of the slice: x: 2, y: 2, z: 4, core: 2. Of those that a mesh axis runs over, the one named last changes fastest.
Arguments:
- inputs: bfloat16 [32768, 768], P(('dp', 'mp')), may hold values from -6 to 6
- lengths: int32 [32], P(('dp', 'mp')), may hold values from 102 to 1024, as said below
- attn_qkv: bfloat16 [1, 768, 2304], P(None, ('dp', 'mp')), may hold values from -0.21875 to 0.21875
- attn_proj: bfloat16 [1, 768, 768], P(None, ('dp', 'mp')), may hold values from -1.75 to 1.75
- mlp_in: bfloat16 [1, 768, 3072], P(None, 'dp', 'mp'), may hold values from -0.21875 to 0.21875
- mlp_out: bfloat16 [1, 3072, 768], P(None, 'mp', 'dp'), may hold values from -0.109375 to 0.109375
- norm_gain: bfloat16 [1, 2, 768], P(None, None, ('dp', 'mp')), may hold values from 0.099609375 to 1.8984375
- norm_bias: bfloat16 [1, 2, 768], P(None, None, ('dp', 'mp')), may hold values from -1.5 to 1.5
- cotangent: bfloat16 [32768, 768], P(('dp', 'mp')), may hold values from -6 to 6
Outputs:
- outputs: bfloat16 [32768, 768], P(('dp', 'mp'))
- input_grad: float32 [32768, 768], P(('dp', 'mp'))
- qkv_grad: float32 [1, 768, 2304], P(None, ('dp', 'mp'))
- proj_grad: float32 [1, 768, 768], P(None, ('dp', 'mp'))
- mlp_in_grad: float32 [1, 768, 3072], P(None, 'dp', 'mp')
- mlp_out_grad: float32 [1, 3072, 768], P(None, 'mp', 'dp')
- gain_grad: float32 [1, 2, 768], P(None, None, ('dp', 'mp'))
- bias_grad: float32 [1, 2, 768], P(None, None, ('dp', 'mp'))
Inputs may be any that keep to these rules, and one draw needn't show every extreme that they name: `lengths`: the true patch count of each clip; slots at or beyond it are padding. Some clip has 1024 patches and some has 102.
All inputs are finite; a program needn't handle non-finite values.
Results may differ from a plain program's by a relative error of at most 0.011.
Values may be sent and summed in bfloat16 or wider, within the bound.
A program may use at most 320 MiB of HBM per device.

v0:
```python
import functools

import jax
import jax.numpy as jnp
from jax import lax
from jax.experimental import pallas as pl
from jax.experimental.pallas import tpu as pltpu
from jax.sharding import PartitionSpec as P

F32, BF = jnp.float32, jnp.bfloat16
MESH = pl.DeviceIdType.MESH
HEAD_DIM = 64
SCALE = 0.125
LOG2E = 1.4426950408889634
TO_LOG2 = SCALE * LOG2E
NEG = -1e30
EPS = 1e-06
NN = (((1,), (0,)), ((), ()))
NT = (((1,), (1,)), ((), ()))
TN = (((0,), (0,)), ((), ()))
VMEM_LIMIT = 60 * 2**20
ANY = pl.BlockSpec(memory_space=pl.ANY)
VMEM = pl.BlockSpec(memory_space=pltpu.VMEM)
SMEM = pl.BlockSpec(memory_space=pltpu.SMEM)
DMA = pltpu.SemaphoreType.DMA


def dot(a, b, dims):
    return lax.dot_general(a, b, dims, preferred_element_type=F32)


def params_of(collective_id=None, grid=0):
    extra = {} if collective_id is None else {"collective_id": collective_id, "has_side_effects": True}
    if grid:
        extra["dimension_semantics"] = ("arbitrary",) * grid
    return pltpu.CompilerParams(vmem_limit_bytes=VMEM_LIMIT, **extra)


class Place:
    def __init__(self, everyone=False):
        self.everyone = everyone
        n_dp, self.M = lax.axis_size("dp"), lax.axis_size("mp")
        self.G = n_dp // 2
        dp = lax.axis_index("dp")
        self.g, self.c, self.z = dp // 2, lax.rem(dp, 2), lax.axis_index("mp")
        self.square = self.G == 4
        near = [sorted(range(self.M), key=lambda s: (abs(s - z), s)) for z in range(self.M)]
        self.near = [sum(jnp.where(self.z == z, near[z][n], 0) for z in range(self.M)) for n in range(self.M)]
        if self.square:
            self.chips = [self.g ^ 1, self.g ^ 2]
            self.diag = self.g ^ 3
        else:
            self.chips = [lax.rem(self.g + d, self.G) for d in range(1, self.G)]

    def chip(self, h):
        return (h * 2 + self.c, self.z)

    def core(self):
        return (self.g * 2 + 1 - self.c, self.z)

    def along(self, z):
        return (self.g * 2 + self.c, z)

    def peers(self):
        if self.everyone:
            n = 2 * self.G * self.M
            return [self.device(lax.rem(self.index + d, n)) for d in range(1, n)]
        return [self.along(s) for s in self.near[1:]] + [self.chip(h) for h in self.chips] + [self.core()]

    @property
    def index(self):
        return (self.g * 2 + self.c) * self.M + self.z

    def device(self, i):
        return (i // self.M, lax.rem(i, self.M))

    def greet(self):
        for dev in self.peers():
            pl.semaphore_signal(pltpu.get_barrier_semaphore(), inc=1, device_id=dev, device_id_type=MESH)

    def meet(self):
        pl.semaphore_wait(pltpu.get_barrier_semaphore(), len(self.peers()))


def remote(src, dst, send, recv, dev):
    return pltpu.make_async_remote_copy(src_ref=src, dst_ref=dst, send_sem=send, recv_sem=recv, device_id=dev, device_id_type=MESH)


class Chain:
    def __init__(self, at, own, land, sends, recvs):
        self.at, self.own, self.land, self.sends, self.recvs = at, own, land, sends, recvs
        self.up, self.down = at.z < at.M - 1, at.z > 0

    def _copy(self, k, src, s, z):
        return remote(src, self.land(s), self.sends.at[k], self.recvs.at[s], self.at.along(z))

    def _own(self, act):
        at = self.at
        for k, (ok, z) in enumerate(((self.up, at.z + 1), (self.down, at.z - 1))):
            pl.when(ok)(lambda k=k, z=z: act(self._copy(k, self.own, at.z, z)))

    def _pass(self, n, act):
        at, s = self.at, self.at.near[n]
        block = self.land(s)
        pl.when((s > at.z) & self.down)(lambda: act(self._copy(1 + n, block, s, at.z - 1)))
        pl.when((s < at.z) & self.up)(lambda: act(self._copy(1 + n, block, s, at.z + 1)))

    def start(self):
        self._own(lambda cp: cp.start())

    def arrive(self, n):
        s = self.at.near[n]
        self._copy(1 + n, self.land(s), s, self.at.z).wait_recv()
        if self.at.M > 2:
            self._pass(n, lambda cp: cp.start())

    def finish(self):
        self._own(lambda cp: cp.wait_send())
        if self.at.M > 2:
            for n in range(1, self.at.M):
                self._pass(n, lambda cp: cp.wait_send())


class GatherUnit:
    def __init__(self, at, src, slot, way, sends, recvs, local=True):
        self.at, self.src, self.slot, self.way, self.local = at, src, slot, way, local
        self.sends, self.recvs = sends, recvs

    @staticmethod
    def count(G):
        return 1 + (3 if G == 4 else G - 1) + G

    def _local(self):
        return pltpu.make_async_copy(self.src, self.slot(self.at.g, self.at.c), self.sends.at[0])

    def _to_chip(self, i):
        at = self.at
        return remote(self.src, self.slot(at.g, at.c), self.sends.at[1 + i], self.recvs.at[1 + i], at.chip(at.chips[i]))

    def _relay(self):
        at = self.at
        block = self.slot(at.chips[self.way], at.c)
        return remote(block, block, self.sends.at[3], self.recvs.at[3], at.chip(at.chips[1 - self.way]))

    def _to_core(self, i):
        at = self.at
        h = ([at.g] + at.chips + ([at.diag] if at.square else []))[i]
        k = self.count(at.G) - at.G + i
        block = self.slot(h, at.c)
        return remote(block if i else self.src, block, self.sends.at[k], self.recvs.at[k], at.core())

    def spread(self):
        for i in range(len(self.at.chips)):
            self._to_chip(i).start()
        self._to_core(0).start()
        if self.local:
            self._local().start()

    def relay(self):
        n = len(self.at.chips)
        for i in range(n):
            self._to_chip(i).wait_recv()
        if self.at.square:
            self._relay().start()
        for i in range(n):
            self._to_core(1 + i).start()

    def last(self):
        if self.at.square:
            self._relay().wait_recv()
            self._to_core(3).start()

    def finish(self):
        if self.local:
            self._local().wait()
        for i in range(len(self.at.chips)):
            self._to_chip(i).wait_send()
        if self.at.square:
            self._relay().wait_send()
        for i in range(self.at.G):
            self._to_core(i).wait()


class SumUnit:
    def __init__(self, at, part, own, got, near, diag, out, far, total, n, way, sends, recvs, far_recvs, local=False):
        self.at, self.part, self.own, self.got, self.near, self.diagonal = at, part, own, got, near, diag
        self.out, self.far, self.total, self.n, self.way = out, far, total, n, way
        self.sends, self.recvs, self.far_recvs, self.local = sends, recvs, far_recvs, local
        self.place = at.near[n]

    @staticmethod
    def count(G):
        return 3 + (3 if G == 4 else G)

    def _core(self):
        at = self.at
        return remote(self.part(1 - at.c), self.got, self.sends.at[0], self.recvs.at[0], at.core())

    def _local(self):
        return pltpu.make_async_copy(self.part(self.at.c), self.own, self.sends.at[2])

    def _diag(self):
        at = self.at
        return remote(self.got.at[at.diag], self.diagonal, self.sends.at[5], self.recvs.at[5], at.chip(at.chips[1 - self.way]))

    def _chip(self, i):
        at = self.at
        k = 3 + i
        return remote(self.got.at[at.chips[i]], self.near.at[i], self.sends.at[k], self.recvs.at[k], at.chip(at.chips[i]))

    def _z(self, source):
        return remote(self.out, self.far.at[source], self.sends.at[1], self.far_recvs.at[source], self.at.along(self.place))

    def start(self):
        self._core().start()
        if self.local:
            self._local().start()

    def pair(self):
        at = self.at
        self._core().wait_recv()
        if self.local:
            self._local().wait()
            own = self.own
        else:
            own = self.part(at.c)
        self.got[...] = (self.got[...].astype(F32) + own[...].astype(F32)).astype(BF)
        if at.square:
            self._diag().start()
        else:
            for i in range(len(at.chips)):
                self._chip(i).start()

    def cross(self):
        at = self.at
        if at.square:
            self._diag().wait_recv()
            h = at.chips[self.way]
            self.got[h] = (self.got[h].astype(F32) + self.diagonal[...].astype(F32)).astype(BF)
            for i in range(2):
                self._chip(i).start()

    def join(self):
        at = self.at
        value = self.got[at.g].astype(F32)
        for i in range(len(at.chips)):
            self._chip(i).wait_recv()
            value = value + self.near[i].astype(F32)
        if self.n:
            self.out[...] = value.astype(BF)
            self._z(self.at.z).start()
        else:
            self.total[...] = value

    def close(self):
        if self.n:
            self._z(self.place).wait_recv()
            self.total[...] += self.far[self.place].astype(F32)

    def finish(self):
        at = self.at
        self._core().wait_send()
        if self.n:
            self._z(at.z).wait_send()
        for i in range(len(at.chips)):
            self._chip(i).wait_send()
        if at.square:
            self._diag().wait_send()


def sum_buffers(n, G, shape, own=True, far=0):
    chips = 2 if G == 4 else G - 1
    block = lambda *lead: pltpu.VMEM(lead + shape, BF)
    return ([block(n, G)] if own else []) + [block(n, G), block(n, chips), block(n), block(n), block(max(far, 1))]


class SmallSum:
    def __init__(self, at, have, got, sends, recvs):
        self.at, self.have, self.got, self.sends, self.recvs = at, have, got, sends, recvs
        hops = [[at.along(s) for s in at.near[1:]]]
        if at.square:
            hops += [[at.chip(h)] for h in at.chips]
        else:
            hops += [[at.chip(h) for h in at.chips]]
        self.hops = hops + [[at.core()]]

    @staticmethod
    def counts(G, M):
        return (5 if G == 4 else 4), M + (2 if G == 4 else G - 1) + 1

    def _copies(self, s, back=False):
        at = self.at
        base = at.M + sum(len(h) for h in self.hops[1:s]) if s else 0
        slots = [base + i for i in range(len(self.hops[s]))]
        if s == 0:
            slots = at.near[1:] if back else [at.z] * (at.M - 1)
        return [
            remote(self.have.at[s], self.got.at[k], self.sends.at[base + i], self.recvs.at[k], dev)
            for i, (k, dev) in enumerate(zip(slots, self.hops[s]))
        ], slots

    def stage(self, s):
        if s:
            copies, slots = self._copies(s - 1, True)
            value = self.have[s - 1]
            for k, cp in zip(slots, copies):
                cp.wait_recv()
                value = value + self.got[k]
            self.have[s] = value
        if s < len(self.hops):
            for cp in self._copies(s)[0]:
                cp.start()

    def finish(self):
        for s in range(len(self.hops)):
            for cp in self._copies(s)[0]:
                cp.wait_send()


class SmallScatter:
    def __init__(self, at, parts, got, sends, recvs):
        self.at, self.parts, self.got, self.sends, self.recvs = at, parts, got, sends, recvs
        self.count = 2 * at.G * at.M

    def _copy(self, d, back):
        at = self.at
        to, other = lax.rem(at.index + d, self.count), lax.rem(at.index + self.count - d, self.count)
        return remote(self.parts.at[to], self.got.at[other if back else at.index], self.sends.at[d], self.recvs.at[d], at.device(to))

    def start(self, value, R):
        for i in range(self.count):
            self.parts[i] = (pltpu.roll(value, value.shape[1] - i * R, 1) if i else value)[:, :128]

        def send(d, carry):
            self._copy(d, False).start()
            return carry

        lax.fori_loop(1, self.count, send, 0)

    def collect(self):
        def add(d, value):
            self._copy(d, True).wait_recv()
            return value + self.got[lax.rem(self.at.index + self.count - d, self.count)]

        return lax.fori_loop(1, self.count, add, self.parts[self.at.index])

    def finish(self):
        def wait(d, carry):
            self._copy(d, False).wait_send()
            return carry

        lax.fori_loop(1, self.count, wait, 0)


def norm_stats(v):
    centre = v - jnp.mean(v, axis=-1, keepdims=True)
    r = lax.rsqrt(jnp.mean(centre * centre, axis=-1, keepdims=True) + EPS)
    return centre * r, r


def norm_pull(e, xhat, r, g):
    y = e * g
    return r * (y - jnp.mean(y, axis=-1, keepdims=True) - xhat * jnp.mean(y * xhat, axis=-1, keepdims=True))


def entry_kernel(x_ref, shard_ref, placed_ref, w_ref, normed_ref, params_ref, have, got, chain_sends, chain_recvs, sends, recvs,
                 small_sends, small_recvs, *, rows):
    at = Place()
    at.greet()
    have[0] = placed_ref[...]
    land = lambda s: w_ref.at[:, at.g, at.c, s]
    chain = Chain(at, shard_ref, land, chain_sends, chain_recvs)
    units = [
        GatherUnit(at, land(at.near[n]) if n else shard_ref, lambda g, c, n=n: w_ref.at[:, g, c, at.near[n]], n % 2, sends.at[n], recvs.at[n], n == 0)
        for n in range(at.M)
    ]
    small = SmallSum(at, have, got, small_sends, small_recvs)
    last = len(small.hops)
    at.meet()
    chain.start()
    units[0].spread()
    small.stage(0)
    stage = 1
    for n in range(1, at.M + 2):
        if n < at.M:
            chain.arrive(n)
            units[n].spread()
        if n - 1 < at.M:
            units[n - 1].relay()
        if stage <= last:
            small.stage(stage)
            stage += 1
        if 0 <= n - 2 < at.M:
            units[n - 2].last()
    while stage <= last:
        small.stage(stage)
        stage += 1
    params_ref[...] = have[last]
    gain, bias = have[last, 0:1, :], have[last, 2:3, :]

    def norm(i, carry):
        sl = pl.ds(pl.multiple_of(i * rows, rows), rows)
        xhat, _ = norm_stats(x_ref[sl, :].astype(F32))
        normed_ref[sl, :] = (xhat * gain + bias).astype(BF)
        return carry

    lax.fori_loop(0, x_ref.shape[0] // rows, norm, 0)
    for u in units:
        u.finish()
    chain.finish()
    small.finish()


def entry(x, shard, placed):
    at_G, M = lax.axis_size("dp") // 2, lax.axis_size("mp")
    L, D = x.shape
    n_have, n_got = SmallSum.counts(at_G, M)
    sems = (M, GatherUnit.count(at_G))
    return pl.pallas_call(
        functools.partial(entry_kernel, rows=min(256, L)),
        in_specs=[VMEM, ANY, VMEM],
        out_specs=[ANY, VMEM, VMEM],
        out_shape=[
            jax.ShapeDtypeStruct((3, at_G, 2, M) + shard.shape[1:], BF),
            jax.ShapeDtypeStruct((L, D), BF),
            jax.ShapeDtypeStruct(placed.shape, F32),
        ],
        scratch_shapes=[
            pltpu.VMEM((n_have,) + placed.shape, F32),
            pltpu.VMEM((n_got,) + placed.shape, F32),
            DMA((M + 1,)), DMA((M,)), DMA(sems), DMA(sems), DMA((n_got,)), DMA((n_got,)),
        ],
        compiler_params=params_of(0),
    )(x, shard, placed)


def lanes(shape):
    return lax.broadcasted_iota(jnp.int32, shape, len(shape) - 1)


def three_parts(x):
    hi = x.astype(BF)
    rest = x - hi.astype(F32)
    mid = rest.astype(BF)
    return hi, mid, (rest - mid.astype(F32)).astype(BF)


def mask_bias(shape, length):
    return jnp.where(lax.broadcasted_iota(jnp.int32, shape, 0) < length, 0.0, NEG).astype(BF)


def attend_step(p, len_ref, q_ref, k_ref, v_ref, o_ref, wide_ref, lse_ref, tq, between):
    L = q_ref.shape[0]
    lane = lanes((L, 128))
    k, v = k_ref[...], v_ref[...]
    bias = mask_bias((L, 128), len_ref[0])
    zero, one = jnp.zeros((L, 128), BF), jnp.ones((L, 128), BF)

    @pl.when(p == 0)
    def _():
        lse_ref[...] = jnp.zeros_like(lse_ref)

    keys, values = [], []
    for h in range(2):
        mine = (lane < 64) if h == 0 else (lane >= 64)
        spare = 64 * (1 - h)
        keys.append(jnp.where(mine, k, jnp.where(lane == spare, bias, zero)))
        values.append(jnp.where(mine, v, jnp.where(lane == spare, one, zero)))
    lq = lanes((tq, 128))
    for i in range(L // tq):
        between(i)
        sl = pl.ds(i * tq, tq)
        q = q_ref[sl, :]
        outs, sums = [], []
        for h in range(2):
            mine = (lq < 64) if h == 0 else (lq >= 64)
            spare = 64 * (1 - h)
            q_h = jnp.where(mine, q, jnp.where(lq == spare, jnp.ones((tq, 128), BF), jnp.zeros((tq, 128), BF)))
            s = dot(q_h, keys[h], NT)
            top = jnp.max(s, axis=1, keepdims=True) * TO_LOG2
            e = jnp.exp2(s * TO_LOG2 - top)
            o = dot(e.astype(BF), values[h], NN)
            total = o[:, spare : spare + 1]
            outs.append(o / total)
            sums.append(top + jnp.log2(total))
        out = jnp.where(lq < 64, outs[0], outs[1])
        wide_ref[sl, :] = out
        o_ref[sl, :] = out.astype(BF)
        lse = lse_ref[sl, :]
        lse = jnp.where(lq == 2 * p, sums[0], lse)
        lse_ref[sl, :] = jnp.where(lq == 2 * p + 1, sums[1], lse)


def attend_back_step(p, len_ref, q_ref, k_ref, v_ref, do_ref, wide_ref, lse_ref, dq_ref, dk_ref, dv_ref, tq, between):
    L = q_ref.shape[0]
    lane = lanes((L, 128))
    k, v = k_ref[...], v_ref[...]
    bias = mask_bias((L, 128), len_ref[0])
    zero, one = jnp.zeros((L, 128), BF), jnp.ones((L, 128), BF)
    keys, values = [], []
    for h in range(2):
        mine = (lane < 64) if h == 0 else (lane >= 64)
        b = 64 * (1 - h)
        ones = jnp.where((lane > b) & (lane < b + 4), one, zero)
        keys.append(jnp.where(mine, k, jnp.where(lane == b, bias, ones)))
        values.append(jnp.where(mine, v, ones))
    lq = lanes((tq, 128))
    dk, dv = [jnp.zeros((L, 128), F32)] * 2, [jnp.zeros((L, 128), F32)] * 2
    for i in range(L // tq):
        between(i)
        sl = pl.ds(i * tq, tq)
        q, do, lse = q_ref[sl, :], do_ref[sl, :], lse_ref[sl, :]
        product = wide_ref[sl, :] * do.astype(F32)
        dq = []
        for h in range(2):
            mine = (lq < 64) if h == 0 else (lq >= 64)
            b = 64 * (1 - h)
            minus_delta = -jnp.sum(jnp.where(mine, product, 0.0), axis=1, keepdims=True)
            minus_lse = -jnp.sum(jnp.where(lq == 2 * p + h, lse, 0.0), axis=1, keepdims=True) * (1.0 / TO_LOG2)

            def with_spare(x, term, first):
                hi, mid, lo = three_parts(jnp.broadcast_to(term, (tq, 128)))
                low = jnp.where(lq == b + 2, mid, jnp.where(lq == b + 3, lo, jnp.zeros((tq, 128), BF)))
                low = jnp.where(lq == b, jnp.full((tq, 128), first, BF), jnp.where(lq == b + 1, hi, low))
                return jnp.where(mine, x, low)

            st = dot(keys[h], with_spare(q, minus_lse, 1.0), NT)
            pt = jnp.exp2(st * TO_LOG2)
            dpt = dot(values[h], with_spare(do, minus_delta, 0.0), NT)
            ds = (pt * dpt).astype(BF)
            dv[h] = dv[h] + dot(pt.astype(BF), do, NN)
            dk[h] = dk[h] + dot(ds, q, NN)
            dq.append(dot(ds, k, TN))
        dq_ref[sl, :] = (jnp.where(lq < 64, dq[0], dq[1]) * SCALE).astype(BF)
    dk_ref[...] = (jnp.where(lane < 64, dk[0], dk[1]) * SCALE).astype(BF)
    dv_ref[...] = jnp.where(lane < 64, dv[0], dv[1]).astype(BF)


def at_slots(p, per_step, plan):
    def between(i):
        for slot, actions in sorted(plan.items()):
            if slot % per_step == i:

                @pl.when(p == slot // per_step)
                def _(actions=actions):
                    for action in actions:
                        action()

    return between


def attend_kernel(len_ref, x_ref, w_ref, proj_ref, io_ref, o_ref, wide_ref, lse_ref, packed_ref, wproj_ref, land_ref, win_ref, wout_ref,
                  packed_s, save_sem, pchain_sends, pchain_recvs, chain_sends, chain_recvs, sends, recvs, *, tq):
    p, steps = pl.program_id(0), pl.num_programs(0)
    at = Place()
    M = at.M
    half = M // 2
    D = x_ref.shape[1]
    parts = x_ref.shape[0] // tq
    land = [lambda s, a=a: land_ref.at[s, a] for a in range(2)]
    pland = lambda s: wproj_ref.at[at.g, at.c, s]
    pchain = Chain(at, proj_ref, pland, pchain_sends, pchain_recvs)
    chains = [Chain(at, io_ref.at[a], land[a], chain_sends.at[a], chain_recvs.at[a]) for a in range(2)]
    main = [
        [GatherUnit(at, land[a](at.near[n]) if n else io_ref.at[a], lambda g, c, n=n, ref=ref: ref.at[n, g, c], a, sends.at[2 * n + a], recvs.at[2 * n + a])
         for a, ref in enumerate((win_ref, wout_ref))]
        for n in range(half)
    ]
    proj = [
        GatherUnit(at, pland(at.near[n]) if n else proj_ref, lambda g, c, n=n: wproj_ref.at[g, c, at.near[n]], n % 2,
                   sends.at[2 * half + n], recvs.at[2 * half + n], n == 0)
        for n in range(M)
    ]
    own_land = [pltpu.make_async_copy(io_ref.at[a], land_ref.at[at.z, a], save_sem.at[1 + a]) for a in range(2)]
    save = pltpu.make_async_copy(packed_s, packed_ref, save_sem.at[0])

    def third(t):
        packed_s[:, pl.ds(t * D, D)] = dot(x_ref[...], w_ref[t], NN).astype(BF)

    @pl.when(p == 0)
    def _():
        at.greet()
        third(0)
        at.meet()
        pchain.start()
        for chain in chains:
            chain.start()
        proj[0].spread()
        for u in main[0]:
            u.spread()
        for cp in own_land:
            cp.start()
        third(1)
        third(2)
        save.start()

    plan = {}

    def put(slot, *actions):
        plan.setdefault(min(slot, ATTEND_STEPS * parts - 1), []).extend(actions)

    def arrive(chain, n, unit=None):
        def act():
            chain.arrive(n)
            if unit is not None:
                unit.spread()

        return act

    for n in range(1, M):
        put(2 * n - 2, arrive(pchain, n, proj[n]))
        for a in range(2):
            put(3 * n - 2 + a, arrive(chains[a], n, main[n][a] if n < half else None))
    put(1, main[0][0].relay, main[0][1].relay)
    for n in range(M):
        put(2 + 2 * n, proj[n].relay)
        put(4 + 2 * n, proj[n].last)
    put(4, main[0][0].last, main[0][1].last)
    for n in range(1, half):
        put(4 + 2 * n, main[n][0].relay)
        put(5 + 2 * n, main[n][1].relay)
        put(8 + n, main[n][0].last, main[n][1].last)
    lane = pl.multiple_of(p * 128, 128)
    column = lambda t: packed_s.at[:, pl.ds(t * D + lane, 128)]
    attend_step(p, len_ref, column(0), column(1), column(2), o_ref, wide_ref, lse_ref, tq, at_slots(p, parts, plan))

    @pl.when(p == steps - 1)
    def _():
        for group in main + [proj, chains, [pchain]]:
            for u in group:
                u.finish()
        save.wait()
        for cp in own_land:
            cp.wait()


ATTEND_STEPS = 6


def attend(lengths, x, w, proj, io, tq):
    G, M = lax.axis_size("dp") // 2, lax.axis_size("mp")
    L, D = x.shape
    half = M // 2
    column = pl.BlockSpec((L, 128), lambda p: (0, p))
    whole = lambda shape: pl.BlockSpec(shape, lambda p: (0,) * len(shape), pipeline_mode=pl.Buffered(1))
    sems = (2 * half + M, GatherUnit.count(G))
    weights = jax.ShapeDtypeStruct((half, G, 2) + io.shape[1:], BF)
    return pl.pallas_call(
        functools.partial(attend_kernel, tq=tq),
        grid=(D // 128,),
        in_specs=[SMEM, whole(x.shape), whole(w.shape), ANY, ANY],
        out_specs=[column, column, pl.BlockSpec((L, 128), lambda p: (0, 0)), ANY, ANY, ANY, ANY, ANY],
        out_shape=[
            jax.ShapeDtypeStruct((L, D), BF),
            jax.ShapeDtypeStruct((L, D), F32),
            jax.ShapeDtypeStruct((L, 128), F32),
            jax.ShapeDtypeStruct((L, 3 * D), BF),
            jax.ShapeDtypeStruct((G, 2, M) + proj.shape, BF),
            jax.ShapeDtypeStruct((M,) + io.shape, BF),
            weights, weights,
        ],
        scratch_shapes=[pltpu.VMEM((L, 3 * D), BF), DMA((3,)), DMA((M + 1,)), DMA((M,)), DMA((2, M + 1)), DMA((2, M)), DMA(sems), DMA(sems)],
        compiler_params=params_of(1, grid=1),
    )(lengths, x, w, proj, io)


def gelu_and_slope(x):
    phi = 0.5 + 0.5 * lax.erf(x * 0.7071067811865476)
    return x * phi, phi + x * (jnp.exp2((x * x) * (-0.5 * LOG2E)) * 0.3989422804014327)


def mlp_kernel(len_ref, x_ref, mixed_ref, cot_ref, params_ref, wproj_ref, win_ref, wout_ref, land_ref,
               y_ref, mgrad_ref, dmixed_ref, sums_ref, pproj_ref, pin_ref, pout_ref, din_ref, dout_ref,
               w_s, mid_s, hid_s, sg_s, sec_s, br_s, act_s, eg_s, got_s, near_s, diag_s, send_s, far_s,
               load_sems, save_sems, gsends, grecvs, ssends, srecvs, far_recvs, *, tr):
    at = Place()
    G, M = at.G, at.M
    L, D = x_ref.shape
    R, Fb = land_ref.shape[2:]
    half = M // 2
    gain, bias = params_ref[1:2, :], params_ref[3:4, :]
    loads = [pltpu.make_async_copy((win_ref, wout_ref)[a].at[k], w_s.at[k, a], load_sems.at[k, a]) for k in range(half) for a in range(2)]
    for cp in loads:
        cp.start()
    at.greet()
    gathers = [
        [GatherUnit(at, land_ref.at[at.near[k], a], lambda g, c, k=k, a=a: w_s.at[k, a, g * 2 + c], a, gsends.at[k - half, a], grecvs.at[k - half, a])
         for a in range(2)]
        for k in range(half, M)
    ]
    sums = [
        SumUnit(at, lambda c, a=a: w_s.at[0, a, pl.ds(c * G, G)], None, got_s.at[a], near_s.at[a], diag_s.at[a], send_s.at[a], far_s, total, 0, a,
                ssends.at[a], srecvs.at[a], far_recvs)
        for a, total in enumerate((din_ref, dout_ref))
    ]

    def rows(i):
        return pl.ds(i * tr, tr)

    def enter(i):
        sl = rows(i)
        mid = x_ref[sl, :].astype(F32) + dot(mixed_ref[sl, :], wproj_ref[...], NN)
        mid_s[sl, :] = mid
        hid_s[sl, :] = mid
        sec_s[sl, :] = (norm_stats(mid)[0] * gain + bias).astype(BF)
        at_row = lax.broadcasted_iota(jnp.int32, (tr, D), 0) + i * tr
        br_s[sl, :] = jnp.where(at_row < len_ref[0], cot_ref[sl, :].astype(F32), 0.0).astype(BF)
        sg_s[sl, :] = jnp.zeros((tr, D), F32)

    n_rows = L // tr
    enter(0)
    at.meet()
    for group in gathers:
        for u in group:
            u.spread()
    for i in range(1, n_rows):
        enter(i)
    for cp in loads:
        cp.wait()
    per = n_rows + 2
    plan = {}

    def put(k, i, name, group):
        plan.setdefault((min(k, M - 1), min(i, per - 1)), []).extend(getattr(u, name) for u in group)

    for n, group in enumerate(gathers):
        put(n, 2, "relay", group)
        put(n + 1, 1, "last", group)
        put(half + n, 0, "finish", group)
    put(1, 0, "start", sums)
    put(1, 2, "pair", sums)
    put(2, 1, "cross", sums)
    put(3, 1, "join", sums)

    def block(k, carry):
        def between(i):
            for (at_k, at_i), actions in sorted(plan.items(), key=lambda item: item[0]):
                if at_i == i:

                    @pl.when(k == at_k)
                    def _(actions=actions):
                        for action in actions:
                            action()

        between(0)
        win, wout = (w_s[k, a].reshape(D, Fb) for a in range(2))
        for i in range(n_rows):
            if i:
                between(i)
            sl = rows(i)
            value, slope = gelu_and_slope(dot(sec_s[sl, :], win, NN))
            act = value.astype(BF)
            eg = (dot(br_s[sl, :], wout, NN) * slope).astype(BF)
            act_s[sl, :], eg_s[sl, :] = act, eg
            hid_s[sl, :] += dot(act, wout, NT)
            sg_s[sl, :] += dot(eg, win, NT)
        for a, (left, right) in enumerate(((sec_s, eg_s), (br_s, act_s))):
            between(n_rows + a)
            grad = dot(left[...], right[...], TN)
            for g in range(G):
                for c in range(2):
                    row = (g * 2 + c) * R
                    w_s[k, a, c * G + g] = grad[row : row + R, :].astype(BF)

        @pl.when(k > 0)
        def _():
            for a, ref in enumerate((pin_ref, pout_ref)):
                pltpu.make_async_copy(w_s.at[k, a], ref.at[k - 1], save_sems.at[k - 1, a]).start()

        return carry

    lax.fori_loop(0, M, block, 0)
    sums_ref[...] = jnp.zeros_like(sums_ref)
    n_back = L // 256 if L % 256 == 0 else 1
    tb = L // n_back

    def back(i, carry):
        sl = pl.ds(pl.multiple_of(i * tb, tb), tb)
        y_ref[sl, :] = hid_s[sl, :].astype(BF)
        xhat, r = norm_stats(mid_s[sl, :])
        e = sg_s[sl, :]
        sums_ref[1:2, :] += jnp.sum(e * xhat, axis=0, keepdims=True)
        sums_ref[3:4, :] += jnp.sum(e, axis=0, keepdims=True)
        grad = br_s[sl, :].astype(F32) + norm_pull(e, xhat, r, gain)
        mgrad_ref[sl, :] = grad
        low = grad.astype(BF)
        sec_s[sl, :] = low
        dmixed_ref[sl, :] = dot(low, wproj_ref[...], NT).astype(BF)
        return carry

    lax.fori_loop(0, n_back, back, 0)
    grad = dot(mixed_ref[...], sec_s[...], TN)
    R_p = pproj_ref.shape[3]
    for g in range(G):
        for c in range(2):
            for z in range(M):
                row = ((g * 2 + c) * M + z) * R_p
                pproj_ref[z, c, g] = grad[row : row + R_p, :].astype(BF)
    for k in range(1, M):
        for a, ref in enumerate((pin_ref, pout_ref)):
            pltpu.make_async_copy(w_s.at[k, a], ref.at[k - 1], save_sems.at[k - 1, a]).wait()
    for u in sums:
        u.finish()


def mlp(lengths, x, mixed, cot, params, wproj, win, wout, land, R_p, tr):
    G, M = lax.axis_size("dp") // 2, lax.axis_size("mp")
    half = M // 2
    L, D = x.shape
    R, Fb = block = land.shape[2:]
    gsems, ssems = (M - half, 2, GatherUnit.count(G)), (2, SumUnit.count(G))
    pieces = jax.ShapeDtypeStruct((M - 1, 2 * G) + block, BF)
    return pl.pallas_call(
        functools.partial(mlp_kernel, tr=tr),
        in_specs=[SMEM, VMEM, VMEM, VMEM, VMEM, VMEM, ANY, ANY, ANY],
        out_specs=[VMEM] * 5 + [ANY, ANY, VMEM, VMEM],
        out_shape=[
            jax.ShapeDtypeStruct((L, D), BF),
            jax.ShapeDtypeStruct((L, D), F32),
            jax.ShapeDtypeStruct((L, D), BF),
            jax.ShapeDtypeStruct(params.shape, F32),
            jax.ShapeDtypeStruct((M, 2, G, R_p, D), BF),
            pieces, pieces,
            jax.ShapeDtypeStruct(block, F32), jax.ShapeDtypeStruct(block, F32),
        ],
        scratch_shapes=[
            pltpu.VMEM((M, 2, 2 * G) + block, BF),
            pltpu.VMEM((L, D), F32), pltpu.VMEM((L, D), F32), pltpu.VMEM((L, D), F32),
            pltpu.VMEM((L, D), BF), pltpu.VMEM((L, D), BF), pltpu.VMEM((L, Fb), BF), pltpu.VMEM((L, Fb), BF),
        ] + sum_buffers(2, G, block, own=False) + [DMA((half, 2)), DMA((M - 1, 2)), DMA(gsems), DMA(gsems), DMA(ssems), DMA(ssems), DMA((1,))],
        compiler_params=params_of(4),
    )(lengths, x, mixed, cot, params, wproj, win, wout, land)


def attend_back_kernel(len_ref, q_ref, k_ref, v_ref, do_ref, wide_ref, lse_ref, pin_ref, pout_ref, pproj_ref, hin_ref, hout_ref,
                       dqkv_ref, din_ref, dout_ref, dproj_ref,
                       own_m, got_m, near_m, diag_m, send_m, far_in, own_p, got_p, near_p, diag_p, send_p, far_p, far_out,
                       sends, recvs, far_recvs, *, tq):
    p, steps = pl.program_id(0), pl.num_programs(0)
    at = Place()
    G, M = at.G, at.M
    parts = q_ref.shape[0] // tq
    units = []

    def add(part, bufs, far, total, n, way, kind):
        k = len(units)
        units.append(SumUnit(at, part, *bufs, far, total, n, way, sends.at[k], recvs.at[k], far_recvs.at[kind], local=True))
        return units[-1]

    main = []
    for n in reversed(range(1, M)):
        main.append([
            add(lambda c, n=n, ref=ref: ref.at[n - 1, pl.ds(c * G, G)], [b.at[2 * (n - 1) + a] for b in (own_m, got_m, near_m, diag_m, send_m)],
                far, total, n, a, a)
            for a, (ref, far, total) in enumerate(((pin_ref, far_in, din_ref), (pout_ref, far_out, dout_ref)))
        ])
    proj = [
        add(lambda c, n=n: pproj_ref.at[at.near[n], c], [b.at[n] for b in (own_p, got_p, near_p, diag_p, send_p)], far_p, dproj_ref, n, n % 2, 2)
        for n in reversed(range(M))
    ]
    plan = {}

    def put(slot, name, group):
        plan.setdefault(min(slot, ATTEND_STEPS * parts - 1), []).extend(getattr(u, name) for u in group)

    def begin():
        din_ref[...], dout_ref[...] = hin_ref[...], hout_ref[...]

    plan[0] = [at.greet, begin, at.meet]
    for group in main + [proj]:
        put(0, "start", group)
    for n, group in enumerate(main):
        put(1 + n, "pair", group)
        put(4 + 2 * n, "cross", group)
        put(10 + 3 * n, "join", group)
    put(5, "pair", proj)
    put(11, "cross", proj)
    put(18, "join", proj)
    for group in main + [proj]:
        put(23, "close", group)
    attend_back_step(p, len_ref, q_ref, k_ref, v_ref, do_ref, wide_ref, lse_ref, dqkv_ref.at[0], dqkv_ref.at[1], dqkv_ref.at[2], tq, at_slots(p, parts, plan))

    @pl.when(p == steps - 1)
    def _():
        for u in units:
            u.finish()


def attend_back(lengths, packed, do, wide, lse, p_in, p_out, p_proj, h_in, h_out, tq):
    G, M = lax.axis_size("dp") // 2, lax.axis_size("mp")
    L, D = do.shape
    pairs = D // 128
    column = lambda off: pl.BlockSpec((L, 128), lambda p, off=off: (0, off + p))
    whole = lambda shape: pl.BlockSpec(shape, lambda p: (0,) * len(shape))
    mshape, pshape = h_in.shape, p_proj.shape[3:]
    rest = 2 * (M - 1)
    sems = (rest + M, SumUnit.count(G))
    return pl.pallas_call(
        functools.partial(attend_back_kernel, tq=tq),
        grid=(pairs,),
        in_specs=[SMEM, column(0), column(pairs), column(2 * pairs), column(0), column(0), whole((L, 128)), ANY, ANY, ANY,
                  whole(mshape), whole(mshape)],
        out_specs=[pl.BlockSpec((3, L, 128), lambda p: (0, 0, p)), whole(mshape), whole(mshape), whole(pshape)],
        out_shape=[jax.ShapeDtypeStruct((3, L, D), BF)]
        + [jax.ShapeDtypeStruct(mshape, F32)] * 2 + [jax.ShapeDtypeStruct(pshape, F32)],
        scratch_shapes=sum_buffers(rest, G, mshape, far=M) + sum_buffers(M, G, pshape, far=M)
        + [pltpu.VMEM((M,) + mshape, BF), DMA(sems), DMA(sems), DMA((3, M))],
        compiler_params=params_of(2, grid=1),
    )(lengths, packed, packed, packed, do, wide, lse, p_in, p_out, p_proj, h_in, h_out)


def exit_kernel(x_ref, normed_ref, dqkv_ref, w_ref, mid_ref, second_ref, params_ref, grad_ref, qkv_ref, norms_ref,
                parts_s, got_s, near_s, diag_s, send_s, far_s, norm_s, small_parts, small_got,
                sends, recvs, far_recvs, small_sends, small_recvs, *, rows):
    at = Place(everyone=True)
    G, M = at.G, at.M
    L, D = x_ref.shape
    R = qkv_ref.shape[0]
    small = SmallScatter(at, small_parts, small_got, small_sends, small_recvs)
    units = []
    for t in range(3):
        units.append([
            SumUnit(at, lambda c, t=t, n=n: parts_s.at[t, at.near[n], c], None, *[b.at[t * M + n] for b in (got_s, near_s, diag_s, send_s)],
                    far_s.at[pl.ds(t * M, M)], qkv_ref.at[:, pl.ds(t * D, D)], n, (n + t) % 2, sends.at[t * M + n], recvs.at[t * M + n], far_recvs.at[t])
            for n in reversed(range(M))
        ])

    def run(t, name):
        for u in units[t]:
            getattr(u, name)()

    gain = params_ref[0:1, :]
    n_norm = L // rows
    norm_plan = {0: [(1, "cross")], 1: [(2, "pair"), (0, "join")], 2: [(2, "cross")], 3: [(1, "join")]}
    third_plan = {0: [], 1: [(0, "pair")], 2: [(0, "cross"), (1, "pair")]}

    def third(t, carry):
        grad = dot(normed_ref[...], dqkv_ref[t], TN)
        for g in range(G):
            for c in range(2):
                for z in range(M):
                    k = ((g * 2 + c) * M + z) * R
                    parts_s[t, z, c, g] = grad[k : k + R, :].astype(BF)
        for i, items in third_plan.items():

            @pl.when(t == i)
            def _(i=i, items=items):
                if i == 0:
                    at.meet()
                run(i, "start")
                for item in items:
                    run(*item)

        return carry

    def norm(i, carry):
        sl = pl.ds(pl.multiple_of(i * rows, rows), rows)
        e = sum(dot(dqkv_ref[t, sl, :], w_ref[t], NT) for t in range(3))
        xhat, r = norm_stats(x_ref[sl, :].astype(F32))
        grad_ref[sl, :] = mid_ref[sl, :] + norm_pull(e, xhat, r, gain)
        norm_s[0:1, :] += jnp.sum(e * xhat, axis=0, keepdims=True)
        norm_s[2:3, :] += jnp.sum(e, axis=0, keepdims=True)
        for j, items in norm_plan.items():
            if j < n_norm:

                @pl.when(i == j)
                def _(items=items):
                    for item in items:
                        run(*item)

        return carry

    at.greet()
    norm_s[...] = second_ref[...]
    lax.fori_loop(0, 3, third, 0)
    lax.fori_loop(0, n_norm, norm, 0)
    small.start(norm_s[...], R)
    for j, items in norm_plan.items():
        if j >= n_norm:
            for item in items:
                run(*item)
    run(2, "join")
    run(0, "close")
    run(1, "close")
    norms_ref[...] = small.collect()
    run(2, "close")
    for t in range(3):
        run(t, "finish")
    small.finish()


def leave(x, normed, dqkv, w, middle_grad, second_sums, params, R):
    G, M = lax.axis_size("dp") // 2, lax.axis_size("mp")
    L, D = x.shape
    n = 2 * G * M
    sems = (3 * M, SumUnit.count(G))
    return pl.pallas_call(
        functools.partial(exit_kernel, rows=min(256, L)),
        in_specs=[VMEM] * 7,
        out_specs=[VMEM] * 3,
        out_shape=[
            jax.ShapeDtypeStruct((L, D), F32),
            jax.ShapeDtypeStruct((R, 3 * D), F32),
            jax.ShapeDtypeStruct((8, 128), F32),
        ],
        scratch_shapes=[pltpu.VMEM((3, M, 2, G, R, D), BF)] + sum_buffers(3 * M, G, (R, D), own=False, far=3 * M)
        + [pltpu.VMEM((8, D), F32), pltpu.VMEM((n, 8, 128), F32), pltpu.VMEM((n, 8, 128), F32),
           DMA(sems), DMA(sems), DMA((3, M)), DMA((n,)), DMA((n,))],
        compiler_params=params_of(3),
    )(x, normed, dqkv, w, middle_grad, second_sums, params)


def per_device(inputs, lengths, attn_qkv, attn_proj, mlp_in, mlp_out, norm_gain, norm_bias, cotangent):
    n_dp, n_mp = lax.axis_size("dp"), lax.axis_size("mp")
    G = n_dp // 2
    L, D = inputs.shape
    R = attn_qkv.shape[1]
    here = (lax.axis_index("dp") * n_mp + lax.axis_index("mp")) * R
    small = jnp.concatenate([norm_gain[0], norm_bias[0]], axis=0).astype(F32)
    placed = lax.dynamic_update_slice(jnp.zeros((8, D), F32), small, (0, here))
    shard = attn_qkv[0].reshape(R, 3, D).transpose(1, 0, 2)
    wqkv, normed, params = entry(inputs, shard, placed)
    wqkv = wqkv.reshape(3, D, D)
    io = jnp.stack([mlp_in[0], mlp_out[0].T])
    mixed, wide, lse, packed, wproj, land, win, wout = attend(lengths, normed, wqkv, attn_proj[0], io, min(512, L))
    pieces = lambda w: w.reshape((w.shape[0], n_dp) + w.shape[3:])
    outputs, middle_grad, mixed_grad, second_sums, p_proj, p_in, p_out, h_in, h_out = mlp(
        lengths, inputs, mixed, cotangent, params, wproj.reshape(D, D), pieces(win), pieces(wout), land, R, min(512, L))
    dqkv, d_in, d_out, d_proj = attend_back(
        lengths, packed, mixed_grad, wide, lse, p_in, p_out, p_proj, h_in, h_out, min(256, L))
    input_grad, d_qkv, norms = leave(inputs, normed, dqkv, wqkv, middle_grad, second_sums, params, R)
    return (
        outputs,
        input_grad,
        d_qkv[None],
        d_proj[None],
        d_in[None],
        d_out.T[None],
        norms[None, :2, :R],
        norms[None, 2:4, :R],
    )


def solution(mesh):
    everywhere = ("dp", "mp")
    wide, columns, vector = P(everywhere, None), P(None, everywhere, None), P(None, None, everywhere)
    return jax.shard_map(
        per_device,
        mesh=mesh,
        in_specs=(wide, P(everywhere), columns, columns, P(None, "dp", "mp"), P(None, "mp", "dp"), vector, vector, wide),
        out_specs=(wide, wide, columns, columns, P(None, "dp", "mp"), P(None, "mp", "dp"), vector, vector),
        check_vma=False,
    )
```

profile of v0, /device:TPU:0, one launch (start us, length us, event | category | flops | bytes accessed | tf_op | source)
XLA Modules:
  0.0 251.5 jit_solution(14736987658531839983)
XLA Ops:
  1.3 0.7 maximum_convert_fusion
  2.0 0.4 dynamic_update_slice.3.placed_ref
  2.4 0.0 copy-start.5
  2.4 1.0 reshape_squeeze.3
  3.3 0.7 copy.19
  4.0 1.7 pad_maximum_fusion.io_ref
  5.7 0.0 copy-done.5
  5.7 35.2 %shard_map.152 = (bf16[3,4,2,4,24,768]{5,4,3,2,1,0:T(8,128)(2,1)}, bf16[1024,768]{1,0:T(8,128)(2,1)}, f32[8,768]{1,0:T(8,128)}) custom-call(bf16[1024,768]{1,0:T(8,128)(2,1)} %x_ref.5, bf16[3,24,768]{2,1,0:T(8,128)(2,1)} %bitcast.30, f32[8,768]{1,0:T(8,128)} %copy-done.5), custom_call_target="tpu_custom_call" | custom-call | tf_op jit(solution)/shard_map/pallas_call | solution.py:419
  40.9 51.3 %shard_map.153 = (bf16[1024,768]{1,0:T(8,128)(2,1)}, f32[1024,768]{1,0:T(8,128)}, f32[1024,128]{1,0:T(8,128)}, bf16[1024,2304]{1,0:T(8,128)(2,1)}, bf16[4,2,4,24...) custom-call(s32[1]{0:T(128)S(6)} %copy.27.len_ref, ...), custom_call_target="tpu_custom_call" | custom-call | tf_op jit(solution)/shard_map/pallas_call | solution.py:648
  92.3 54.8 %shard_map.154 = (bf16[1024,768]{1,0:T(8,128)(2,1)}, f32[1024,768]{1,0:T(8,128)}, bf16[1024,768]{1,0:T(8,128)(2,1)}, f32[8,768]{1,0:T(8,128)}, bf16[4,2,4,24,768...) custom-call(s32[1]{0:T(128)S(6)} %copy.27.len_ref, ...), custom_call_target="tpu_custom_call" | custom-call | tf_op jit(solution)/shard_map/pallas_call | solution.py:813
  147.1 57.9 %shard_map.155 = (bf16[3,1024,768]{2,1,0:T(8,128)(2,1)}, f32[96,768]{1,0:T(8,128)}, f32[96,768]{1,0:T(8,128)}, f32[24,768]{1,0:T(8,128)}) custom-call(s32[1]{0:T(128)S(6)} %copy.27.len_ref, bf16[1024,2304]{1,0:T(8,128)(2,1)} %get-tuple-element.44.q_ref.k_ref.v_ref, bf16[1024,2304]{1,0:T(8,128)(2,1)} %get-tuple-element.44.q_ref.k_ref.v_ref, ...), custom_call_target="tpu_custom_call" | custom-call | tf_op jit(solution)/shard_map/pallas_call | solution.py:898
  205.0 0.0 copy-start.1
  205.0 39.4 %shard_map.156 = (f32[1024,768]{1,0:T(8,128)}, f32[24,2304]{1,0:T(8,128)}, f32[8,128]{1,0:T(8,128)}) custom-call(bf16[1024,768]{1,0:T(8,128)(2,1)} %x_ref.5, bf16[1024,768]{1,0:T(8,128)(2,1)} %get-tuple-element.35.x_ref.normed_ref, bf16[3,1024,768]{2,1,0:T(8,128)(2,1)} %get-tuple-element.53.dqkv_ref, bf16[3,768,768]{2,1,0:T(8,128)(2,1)} %bitcast.26, ...), custom_call_target="tpu_custom_call" | custom-call | tf_op jit(solution)/shard_map/pallas_call | solution.py:997
  244.4 0.0 copy-start
  244.5 1.4 slice_bitcast_fusion
  245.9 0.0 copy-done.1
  245.9 1.1 copy.28
  247.0 0.0 copy-done
  247.0 0.0 copy-start.4
  247.0 0.0 copy-start.6
  247.0 0.0 copy-start.3
  247.0 0.0 copy-start.2
  247.0 1.7 copy.29
  248.7 0.0 copy-done.4
  248.7 0.7 copy.30
  249.4 0.0 copy-done.6
  249.4 0.6 copy.31
  250.0 0.0 copy-done.3
  250.0 0.7 copy.32
  250.7 0.0 copy-done.2
  250.7 0.7 copy.33
  (1 shorter events, 0.0 us)
Async XLA Ops:
  2.4 3.4 %copy-start.5 = (f32[8,768]{1,0:T(8,128)}, f32[8,768]{1,0:T(8,128)S(1)}, u32[]{:S(2)}) copy-start(f32[8,768]{1,0:T(8,128)S(1)} %dynamic_update_slice.3.placed_ref) | copy-start | bytes 73732
  205.0 40.9 %copy-start.1 = (bf16[1024,768]{1,0:T(8,128)(2,1)S(1)}, bf16[1024,768]{1,0:T(8,128)(2,1)}, u32[]{:S(2)}) copy-start(bf16[1024,768]{1,0:T(8,128)(2,1)} %get-tuple-element.72) | copy-start | bytes 4718596
  244.4 2.6 %copy-start = (f32[1024,768]{1,0:T(8,128)S(1)}, f32[1024,768]{1,0:T(8,128)}, u32[]{:S(2)}) copy-start(f32[1024,768]{1,0:T(8,128)} %get-tuple-element.73) | copy-start | bytes 9437188
  247.0 1.7 copy-start.4
  247.0 2.4 copy-start.6
  247.0 3.0 %copy-start.3 = (f32[96,768]{1,0:T(8,128)S(1)}, f32[96,768]{1,0:T(8,128)}, u32[]{:S(2)}) copy-start(f32[96,768]{1,0:T(8,128)} %get-tuple-element.59) | copy-start | bytes 884740
  247.0 3.7 %copy-start.2 = (f32[96,768]{1,0:T(8,128)S(1)}, f32[96,768]{1,0:T(8,128)}, u32[]{:S(2)}) copy-start(f32[96,768]{1,0:T(8,128)} %get-tuple-element.60) | copy-start | bytes 884740
where the time goes:
time: 252 us; the launch traced here: 251 us
  Pallas kernels  239 us (95%)
  local copies, waits for them, and re-layouts  8.98 us (4%)
    pallas_call x1, Pallas kernels, attend_back(): pl.pallas_call(functools.partial(attend_back_kernel, tq=tq), grid=(pairs,...  57.9 us
    pallas_call x1, Pallas kernels, mlp(): pl.pallas_call(functools.partial(mlp_kernel, tr=tr), in_specs=[SMEM, VMEM...  54.8 us
    pallas_call x1, Pallas kernels, attend(): pl.pallas_call(functools.partial(attend_kernel, tq=tq), grid=(D // 128,),...  51.3 us
    pallas_call x1, Pallas kernels, leave(): pl.pallas_call(functools.partial(exit_kernel, rows=min(256, L)), in_specs...  39.4 us
    pallas_call x1, Pallas kernels, entry(): pl.pallas_call(functools.partial(entry_kernel, rows=min(256, L)), in_spec...  35.2 us
    unnamed x20, local copies, waits for them, and re-layouts  5.59 us

commit v1 on v0

--- a/solution.py
+++ b/solution.py
@@ -44,8 +44,7 @@
         dp = lax.axis_index("dp")
         self.g, self.c, self.z = dp // 2, lax.rem(dp, 2), lax.axis_index("mp")
         self.square = self.G == 4
-        near = [sorted(range(self.M), key=lambda s: (abs(s - z), s)) for z in range(self.M)]
-        self.near = [sum(jnp.where(self.z == z, near[z][n], 0) for z in range(self.M)) for n in range(self.M)]
+        self.near = [self.z ^ n if self.M & (self.M - 1) == 0 else lax.rem(self.z + n, self.M) for n in range(self.M)]
         if self.square:
             self.chips = [self.g ^ 1, self.g ^ 2]
             self.diag = self.g ^ 3
@@ -86,39 +85,23 @@
     return pltpu.make_async_remote_copy(src_ref=src, dst_ref=dst, send_sem=send, recv_sem=recv, device_id=dev, device_id_type=MESH)
 
 
-class Chain:
+class Along:
     def __init__(self, at, own, land, sends, recvs):
         self.at, self.own, self.land, self.sends, self.recvs = at, own, land, sends, recvs
-        self.up, self.down = at.z < at.M - 1, at.z > 0
-
-    def _copy(self, k, src, s, z):
-        return remote(src, self.land(s), self.sends.at[k], self.recvs.at[s], self.at.along(z))
-
-    def _own(self, act):
-        at = self.at
-        for k, (ok, z) in enumerate(((self.up, at.z + 1), (self.down, at.z - 1))):
-            pl.when(ok)(lambda k=k, z=z: act(self._copy(k, self.own, at.z, z)))
-
-    def _pass(self, n, act):
-        at, s = self.at, self.at.near[n]
-        block = self.land(s)
-        pl.when((s > at.z) & self.down)(lambda: act(self._copy(1 + n, block, s, at.z - 1)))
-        pl.when((s < at.z) & self.up)(lambda: act(self._copy(1 + n, block, s, at.z + 1)))
-
-    def start(self):
-        self._own(lambda cp: cp.start())
+
+    def _copy(self, n, source):
+        return remote(self.own, self.land(source), self.sends.at[n], self.recvs.at[source], self.at.along(self.at.near[n]))
+
+    def start(self, *ns):
+        for n in ns:
+            self._copy(n, self.at.z).start()
 
     def arrive(self, n):
-        s = self.at.near[n]
-        self._copy(1 + n, self.land(s), s, self.at.z).wait_recv()
-        if self.at.M > 2:
-            self._pass(n, lambda cp: cp.start())
+        self._copy(n, self.at.near[n]).wait_recv()
 
     def finish(self):
-        self._own(lambda cp: cp.wait_send())
-        if self.at.M > 2:
-            for n in range(1, self.at.M):
-                self._pass(n, lambda cp: cp.wait_send())
+        for n in range(1, self.at.M):
+            self._copy(n, self.at.z).wait_send()
 
 
 class GatherUnit:
@@ -187,6 +170,8 @@
         self.out, self.far, self.total, self.n, self.way = out, far, total, n, way
         self.sends, self.recvs, self.far_recvs, self.local = sends, recvs, far_recvs, local
         self.place = at.near[n]
+        self.passed = at.M == 4 and n == 3
+        self.opposite = None
 
     @staticmethod
     def count(G):
@@ -208,15 +193,23 @@
         k = 3 + i
         return remote(self.got.at[at.chips[i]], self.near.at[i], self.sends.at[k], self.recvs.at[k], at.chip(at.chips[i]))
 
-    def _z(self, source):
-        return remote(self.out, self.far.at[source], self.sends.at[1], self.far_recvs.at[source], self.at.along(self.place))
+    def _z(self, slot):
+        dev = self.at.along(self.at.near[1] if self.passed else self.place)
+        return remote(self.out, self.far.at[slot], self.sends.at[1], self.far_recvs.at[slot], dev)
+
+    def send_z(self):
+        self._z(self.at.near[2] if self.passed else self.at.z).start()
 
     def start(self):
         self._core().start()
         if self.local:
             self._local().start()
 
-    def pair(self):
+    def launch(self):
+        for i in range(len(self.at.chips)):
+            self._chip(i).start()
+
+    def pair(self, hold=False):
         at = self.at
         self._core().wait_recv()
         if self.local:
@@ -224,21 +217,25 @@
             own = self.own
         else:
             own = self.part(at.c)
-        self.got[...] = (self.got[...].astype(F32) + own[...].astype(F32)).astype(BF)
+
+        def add(h, carry):
+            self.got[h] = (self.got[h].astype(F32) + own[h].astype(F32)).astype(BF)
+            return carry
+
+        lax.fori_loop(0, at.G, add, 0)
         if at.square:
             self._diag().start()
-        else:
-            for i in range(len(at.chips)):
-                self._chip(i).start()
-
-    def cross(self):
+        elif not hold:
+            self.launch()
+
+    def cross(self, hold=False):
         at = self.at
         if at.square:
             self._diag().wait_recv()
             h = at.chips[self.way]
             self.got[h] = (self.got[h].astype(F32) + self.diagonal[...].astype(F32)).astype(BF)
-            for i in range(2):
-                self._chip(i).start()
+            if not hold:
+                self.launch()
 
     def join(self):
         at = self.at
@@ -246,26 +243,38 @@
         for i in range(len(at.chips)):
             self._chip(i).wait_recv()
             value = value + self.near[i].astype(F32)
+        if self.opposite is not None:
+            self._z(at.near[3]).wait_recv()
+            value = value + self.far[at.near[3]].astype(F32)
         if self.n:
             self.out[...] = value.astype(BF)
-            self._z(self.at.z).start()
+            self.send_z()
         else:
             self.total[...] = value
 
     def close(self):
-        if self.n:
+        if self.n and not self.passed:
             self._z(self.place).wait_recv()
             self.total[...] += self.far[self.place].astype(F32)
 
-    def finish(self):
+    def finish(self, core=True, rest=True):
         at = self.at
-        self._core().wait_send()
-        if self.n:
-            self._z(at.z).wait_send()
-        for i in range(len(at.chips)):
-            self._chip(i).wait_send()
-        if at.square:
-            self._diag().wait_send()
+        if core:
+            self._core().wait_send()
+            if at.square:
+                self._diag().wait_send()
+        if rest:
+            if self.n:
+                self._z(at.near[2] if self.passed else at.z).wait_send()
+            for i in range(len(at.chips)):
+                self._chip(i).wait_send()
+
+
+def link(units):
+    by_n = {u.n: u for u in units}
+    if units[0].at.M == 4 and 3 in by_n:
+        by_n[2].opposite = by_n[3]
+    return units
 
 
 def sum_buffers(n, G, shape, own=True, far=0):
@@ -274,47 +283,43 @@
     return ([block(n, G)] if own else []) + [block(n, G), block(n, chips), block(n), block(n), block(max(far, 1))]
 
 
-class SmallSum:
-    def __init__(self, at, have, got, sends, recvs):
-        self.at, self.have, self.got, self.sends, self.recvs = at, have, got, sends, recvs
-        hops = [[at.along(s) for s in at.near[1:]]]
-        if at.square:
-            hops += [[at.chip(h)] for h in at.chips]
-        else:
-            hops += [[at.chip(h) for h in at.chips]]
-        self.hops = hops + [[at.core()]]
-
-    @staticmethod
-    def counts(G, M):
-        return (5 if G == 4 else 4), M + (2 if G == 4 else G - 1) + 1
-
-    def _copies(self, s, back=False):
+class SmallGather:
+    def __init__(self, at, got, sends, recvs):
+        self.at, self.got, self.sends, self.recvs = at, got, sends, recvs
+        self.count = 2 * at.G * at.M
+
+    def _copy(self, own, d, back):
         at = self.at
-        base = at.M + sum(len(h) for h in self.hops[1:s]) if s else 0
-        slots = [base + i for i in range(len(self.hops[s]))]
-        if s == 0:
-            slots = at.near[1:] if back else [at.z] * (at.M - 1)
-        return [
-            remote(self.have.at[s], self.got.at[k], self.sends.at[base + i], self.recvs.at[k], dev)
-            for i, (k, dev) in enumerate(zip(slots, self.hops[s]))
-        ], slots
-
-    def stage(self, s):
-        if s:
-            copies, slots = self._copies(s - 1, True)
-            value = self.have[s - 1]
-            for k, cp in zip(slots, copies):
-                cp.wait_recv()
-                value = value + self.got[k]
-            self.have[s] = value
-        if s < len(self.hops):
-            for cp in self._copies(s)[0]:
-                cp.start()
-
-    def finish(self):
-        for s in range(len(self.hops)):
-            for cp in self._copies(s)[0]:
-                cp.wait_send()
+        to, other = lax.rem(at.index + d, self.count), lax.rem(at.index + self.count - d, self.count)
+        return remote(own, self.got.at[other if back else at.index], self.sends.at[d], self.recvs.at[d], at.device(to))
+
+    def start(self, own):
+        def send(d, carry):
+            self._copy(own, d, False).start()
+            return carry
+
+        lax.fori_loop(1, self.count, send, 0)
+
+    def collect(self, own, R, width):
+        def wait(d, carry):
+            self._copy(own, d, True).wait_recv()
+            return carry
+
+        lax.fori_loop(1, self.count, wait, 0)
+        self.got[self.at.index] = own[...]
+        lane = lanes((own.shape[0], width))
+        total = jnp.zeros((own.shape[0], width), F32)
+        for i in range(self.count):
+            wide = jnp.concatenate([self.got[i]] * (width // 128), axis=1)
+            total = jnp.where(lane // R == i, pltpu.roll(wide, i * R % width, 1) if i else wide, total)
+        return total
+
+    def finish(self, own):
+        def wait(d, carry):
+            self._copy(own, d, False).wait_send()
+            return carry
+
+        lax.fori_loop(1, self.count, wait, 0)
 
 
 class SmallScatter:
@@ -363,75 +368,67 @@
     return r * (y - jnp.mean(y, axis=-1, keepdims=True) - xhat * jnp.mean(y * xhat, axis=-1, keepdims=True))
 
 
-def entry_kernel(x_ref, shard_ref, placed_ref, w_ref, normed_ref, params_ref, have, got, chain_sends, chain_recvs, sends, recvs,
+def entry_kernel(x_ref, shard_ref, own_ref, w_ref, normed_ref, params_ref, got, chain_sends, chain_recvs, sends, recvs,
                  small_sends, small_recvs, *, rows):
-    at = Place()
+    at = Place(everyone=True)
     at.greet()
-    have[0] = placed_ref[...]
     land = lambda s: w_ref.at[:, at.g, at.c, s]
-    chain = Chain(at, shard_ref, land, chain_sends, chain_recvs)
+    chain = Along(at, shard_ref, land, chain_sends, chain_recvs)
     units = [
         GatherUnit(at, land(at.near[n]) if n else shard_ref, lambda g, c, n=n: w_ref.at[:, g, c, at.near[n]], n % 2, sends.at[n], recvs.at[n], n == 0)
         for n in range(at.M)
     ]
-    small = SmallSum(at, have, got, small_sends, small_recvs)
-    last = len(small.hops)
+    small = SmallGather(at, got, small_sends, small_recvs)
+    L, D = x_ref.shape
     at.meet()
-    chain.start()
+    chain.start(1)
     units[0].spread()
-    small.stage(0)
-    stage = 1
-    for n in range(1, at.M + 2):
-        if n < at.M:
-            chain.arrive(n)
-            units[n].spread()
-        if n - 1 < at.M:
-            units[n - 1].relay()
-        if stage <= last:
-            small.stage(stage)
-            stage += 1
-        if 0 <= n - 2 < at.M:
-            units[n - 2].last()
-    while stage <= last:
-        small.stage(stage)
-        stage += 1
-    params_ref[...] = have[last]
-    gain, bias = have[last, 0:1, :], have[last, 2:3, :]
+    chain.start(*range(2, at.M))
+    small.start(own_ref)
 
     def norm(i, carry):
         sl = pl.ds(pl.multiple_of(i * rows, rows), rows)
         xhat, _ = norm_stats(x_ref[sl, :].astype(F32))
-        normed_ref[sl, :] = (xhat * gain + bias).astype(BF)
+        normed_ref[sl, :] = (xhat * params_ref[0:1, :] + params_ref[2:3, :]).astype(BF)
         return carry
 
-    lax.fori_loop(0, x_ref.shape[0] // rows, norm, 0)
+    steps = L // rows
+    for n in range(1, at.M):
+        chain.arrive(n)
+        units[n].spread()
+        units[n - 1].relay()
+        if n > 1:
+            units[n - 2].last()
+    params_ref[...] = small.collect(own_ref, shard_ref.shape[1], D)
+    lax.fori_loop(0, steps // 2, norm, 0)
+    units[-1].relay()
+    if at.M > 1:
+        units[-2].last()
+    lax.fori_loop(steps // 2, steps, norm, 0)
+    units[-1].last()
     for u in units:
         u.finish()
     chain.finish()
-    small.finish()
-
-
-def entry(x, shard, placed):
-    at_G, M = lax.axis_size("dp") // 2, lax.axis_size("mp")
+    small.finish(own_ref)
+
+
+def entry(x, shard, own):
+    G, M = lax.axis_size("dp") // 2, lax.axis_size("mp")
     L, D = x.shape
-    n_have, n_got = SmallSum.counts(at_G, M)
-    sems = (M, GatherUnit.count(at_G))
+    n = 2 * G * M
+    sems = (M, GatherUnit.count(G))
     return pl.pallas_call(
         functools.partial(entry_kernel, rows=min(256, L)),
         in_specs=[VMEM, ANY, VMEM],
         out_specs=[ANY, VMEM, VMEM],
         out_shape=[
-            jax.ShapeDtypeStruct((3, at_G, 2, M) + shard.shape[1:], BF),
+            jax.ShapeDtypeStruct((3, G, 2, M) + shard.shape[1:], BF),
             jax.ShapeDtypeStruct((L, D), BF),
-            jax.ShapeDtypeStruct(placed.shape, F32),
+            jax.ShapeDtypeStruct((8, D), F32),
         ],
-        scratch_shapes=[
-            pltpu.VMEM((n_have,) + placed.shape, F32),
-            pltpu.VMEM((n_got,) + placed.shape, F32),
-            DMA((M + 1,)), DMA((M,)), DMA(sems), DMA(sems), DMA((n_got,)), DMA((n_got,)),
-        ],
+        scratch_shapes=[pltpu.VMEM((n,) + own.shape, F32), DMA((M + 1,)), DMA((M,)), DMA(sems), DMA(sems), DMA((n,)), DMA((n,))],
         compiler_params=params_of(0),
-    )(x, shard, placed)
+    )(x, shard, own)
 
 
 def lanes(shape):
@@ -559,8 +556,8 @@
     parts = x_ref.shape[0] // tq
     land = [lambda s, a=a: land_ref.at[s, a] for a in range(2)]
     pland = lambda s: wproj_ref.at[at.g, at.c, s]
-    pchain = Chain(at, proj_ref, pland, pchain_sends, pchain_recvs)
-    chains = [Chain(at, io_ref.at[a], land[a], chain_sends.at[a], chain_recvs.at[a]) for a in range(2)]
+    pchain = Along(at, proj_ref, pland, pchain_sends, pchain_recvs)
+    chains = [Along(at, io_ref.at[a], land[a], chain_sends.at[a], chain_recvs.at[a]) for a in range(2)]
     main = [
         [GatherUnit(at, land[a](at.near[n]) if n else io_ref.at[a], lambda g, c, n=n, ref=ref: ref.at[n, g, c], a, sends.at[2 * n + a], recvs.at[2 * n + a])
          for a, ref in enumerate((win_ref, wout_ref))]
@@ -582,9 +579,10 @@
         at.greet()
         third(0)
         at.meet()
-        pchain.start()
-        for chain in chains:
-            chain.start()
+        pchain.start(*range(1, M))
+        for n in range(1, M):
+            for chain in chains:
+                chain.start(n)
         proj[0].spread()
         for u in main[0]:
             u.spread()
@@ -608,24 +606,31 @@
         return act
 
     for n in range(1, M):
-        put(2 * n - 2, arrive(pchain, n, proj[n]))
-        for a in range(2):
-            put(3 * n - 2 + a, arrive(chains[a], n, main[n][a] if n < half else None))
-    put(1, main[0][0].relay, main[0][1].relay)
-    for n in range(M):
-        put(2 + 2 * n, proj[n].relay)
-        put(4 + 2 * n, proj[n].last)
-    put(4, main[0][0].last, main[0][1].last)
+        put((1, 4, 6)[min(n, 3) - 1], arrive(pchain, n, proj[n]))
+    put(2, proj[0].relay)
     for n in range(1, half):
-        put(4 + 2 * n, main[n][0].relay)
-        put(5 + 2 * n, main[n][1].relay)
-        put(8 + n, main[n][0].last, main[n][1].last)
+        put(1 + 2 * n, arrive(chains[0], n, main[n][0]))
+        put(2 + 2 * n, arrive(chains[1], n, main[n][1]))
+    put(4, main[0][0].relay, main[0][1].relay)
+    put(5, proj[0].last)
+    for n in range(1, M):
+        put(3 + 2 * n, proj[n].relay)
+        put(min(6 + 2 * n, 11), proj[n].last)
+    for n in range(1, half):
+        put(6 + n, main[n][0].relay)
+        put(7 + n, main[n][1].relay)
+    put(8, main[0][0].last, main[0][1].last)
+    for n in range(1, half):
+        put(10 + n, main[n][0].last, main[n][1].last)
     lane = pl.multiple_of(p * 128, 128)
     column = lambda t: packed_s.at[:, pl.ds(t * D + lane, 128)]
     attend_step(p, len_ref, column(0), column(1), column(2), o_ref, wide_ref, lse_ref, tq, at_slots(p, parts, plan))
 
     @pl.when(p == steps - 1)
     def _():
+        for n in range(half, M):
+            for chain in chains:
+                chain.arrive(n)
         for group in main + [proj, chains, [pchain]]:
             for u in group:
                 u.finish()
@@ -670,9 +675,9 @@
 
 
 def mlp_kernel(len_ref, x_ref, mixed_ref, cot_ref, params_ref, wproj_ref, win_ref, wout_ref, land_ref,
-               y_ref, mgrad_ref, dmixed_ref, sums_ref, pproj_ref, pin_ref, pout_ref, din_ref, dout_ref,
-               w_s, mid_s, hid_s, sg_s, sec_s, br_s, act_s, eg_s, got_s, near_s, diag_s, send_s, far_s,
-               load_sems, save_sems, gsends, grecvs, ssends, srecvs, far_recvs, *, tr):
+               y_ref, mgrad_ref, dmixed_ref, sums_ref, pproj_ref, pin_ref, pout_ref, din_ref, dout_ref, half_ref,
+               w_s, mid_s, hid_s, sg_s, sec_s, br_s, act_s, eg_s, got_s, near_s, diag_s,
+               load_sems, save_sems, gsends, grecvs, ssends, srecvs, *, tr):
     at = Place()
     G, M = at.G, at.M
     L, D = x_ref.shape
@@ -689,9 +694,10 @@
         for k in range(half, M)
     ]
     sums = [
-        SumUnit(at, lambda c, a=a: w_s.at[0, a, pl.ds(c * G, G)], None, got_s.at[a], near_s.at[a], diag_s.at[a], send_s.at[a], far_s, total, 0, a,
-                ssends.at[a], srecvs.at[a], far_recvs)
-        for a, total in enumerate((din_ref, dout_ref))
+        [SumUnit(at, lambda c, k=k, a=a: w_s.at[k, a, pl.ds(c * G, G)], None, *[b.at[2 * k + a] for b in (got_s, near_s, diag_s)], None,
+                 None, total, k, a, ssends.at[2 * k + a], srecvs.at[2 * k + a], None)
+         for a, total in enumerate((din_ref, dout_ref))]
+        for k in range(2)
     ]
 
     def rows(i):
@@ -711,8 +717,9 @@
     enter(0)
     at.meet()
     for group in gathers:
-        for u in group:
-            u.spread()
+        group[0].spread()
+        if group is gathers[0]:
+            group[1].spread()
     for i in range(1, n_rows):
         enter(i)
     for cp in loads:
@@ -723,14 +730,19 @@
     def put(k, i, name, group):
         plan.setdefault((min(k, M - 1), min(i, per - 1)), []).extend(getattr(u, name) for u in group)
 
+    put(0, 3, "relay", gathers[0])
     for n, group in enumerate(gathers):
-        put(n, 2, "relay", group)
-        put(n + 1, 1, "last", group)
+        if n:
+            put(0, 3, "spread", group[1:])
+            put(n, 3, "relay", group)
+        put(n + 1, 2, "last", group)
         put(half + n, 0, "finish", group)
-    put(1, 0, "start", sums)
-    put(1, 2, "pair", sums)
-    put(2, 1, "cross", sums)
-    put(3, 1, "join", sums)
+    put(1, 0, "start", sums[0])
+    put(1, 2, "pair", sums[0])
+    put(2, 0, "start", sums[1])
+    put(2, 1, "cross", sums[0])
+    plan.setdefault((2, 3), []).extend(functools.partial(u.pair, True) for u in sums[1])
+    put(3, 1, "join", sums[0])
 
     def block(k, carry):
         def between(i):
@@ -762,10 +774,10 @@
                     row = (g * 2 + c) * R
                     w_s[k, a, c * G + g] = grad[row : row + R, :].astype(BF)
 
-        @pl.when(k > 0)
+        @pl.when(k > 1)
         def _():
             for a, ref in enumerate((pin_ref, pout_ref)):
-                pltpu.make_async_copy(w_s.at[k, a], ref.at[k - 1], save_sems.at[k - 1, a]).start()
+                pltpu.make_async_copy(w_s.at[k, a], ref.at[k - 2], save_sems.at[k - 2, a]).start()
 
         return carry
 
@@ -789,6 +801,10 @@
         return carry
 
     lax.fori_loop(0, n_back, back, 0)
+    for u in sums[1]:
+        u.cross(True)
+    save_half = pltpu.make_async_copy(got_s.at[pl.ds(2, 2)], half_ref, load_sems.at[0, 0])
+    save_half.start()
     grad = dot(mixed_ref[...], sec_s[...], TN)
     R_p = pproj_ref.shape[3]
     for g in range(G):
@@ -796,11 +812,13 @@
             for z in range(M):
                 row = ((g * 2 + c) * M + z) * R_p
                 pproj_ref[z, c, g] = grad[row : row + R_p, :].astype(BF)
-    for k in range(1, M):
+    for k in range(2, M):
         for a, ref in enumerate((pin_ref, pout_ref)):
-            pltpu.make_async_copy(w_s.at[k, a], ref.at[k - 1], save_sems.at[k - 1, a]).wait()
-    for u in sums:
-        u.finish()
+            pltpu.make_async_copy(w_s.at[k, a], ref.at[k - 2], save_sems.at[k - 2, a]).wait()
+    save_half.wait()
+    for k, group in enumerate(sums):
+        for u in group:
+            u.finish(True, k == 0)
 
 
 def mlp(lengths, x, mixed, cot, params, wproj, win, wout, land, R_p, tr):
@@ -808,12 +826,12 @@
     half = M // 2
     L, D = x.shape
     R, Fb = block = land.shape[2:]
-    gsems, ssems = (M - half, 2, GatherUnit.count(G)), (2, SumUnit.count(G))
-    pieces = jax.ShapeDtypeStruct((M - 1, 2 * G) + block, BF)
+    gsems, ssems = (M - half, 2, GatherUnit.count(G)), (4, SumUnit.count(G))
+    pieces = jax.ShapeDtypeStruct((M - 2, 2 * G) + block, BF)
     return pl.pallas_call(
         functools.partial(mlp_kernel, tr=tr),
         in_specs=[SMEM, VMEM, VMEM, VMEM, VMEM, VMEM, ANY, ANY, ANY],
-        out_specs=[VMEM] * 5 + [ANY, ANY, VMEM, VMEM],
+        out_specs=[VMEM] * 5 + [ANY, ANY, VMEM, VMEM, ANY],
         out_shape=[
             jax.ShapeDtypeStruct((L, D), BF),
             jax.ShapeDtypeStruct((L, D), F32),
@@ -821,193 +839,253 @@
             jax.ShapeDtypeStruct(params.shape, F32),
             jax.ShapeDtypeStruct((M, 2, G, R_p, D), BF),
             pieces, pieces,
-            jax.ShapeDtypeStruct(block, F32), jax.ShapeDtypeStruct(block, F32),
+            jax.ShapeDtypeStruct(block, F32), jax.ShapeDtypeStruct(block, F32), jax.ShapeDtypeStruct((2, G) + block, BF),
         ],
         scratch_shapes=[
             pltpu.VMEM((M, 2, 2 * G) + block, BF),
             pltpu.VMEM((L, D), F32), pltpu.VMEM((L, D), F32), pltpu.VMEM((L, D), F32),
             pltpu.VMEM((L, D), BF), pltpu.VMEM((L, D), BF), pltpu.VMEM((L, Fb), BF), pltpu.VMEM((L, Fb), BF),
-        ] + sum_buffers(2, G, block, own=False) + [DMA((half, 2)), DMA((M - 1, 2)), DMA(gsems), DMA(gsems), DMA(ssems), DMA(ssems), DMA((1,))],
+        ] + sum_buffers(4, G, block, own=False)[:3] + [DMA((half, 2)), DMA((M - 2, 2)), DMA(gsems), DMA(gsems), DMA(ssems), DMA(ssems)],
         compiler_params=params_of(4),
     )(lengths, x, mixed, cot, params, wproj, win, wout, land)
 
 
-def attend_back_kernel(len_ref, q_ref, k_ref, v_ref, do_ref, wide_ref, lse_ref, pin_ref, pout_ref, pproj_ref, hin_ref, hout_ref,
-                       dqkv_ref, din_ref, dout_ref, dproj_ref,
-                       own_m, got_m, near_m, diag_m, send_m, far_in, own_p, got_p, near_p, diag_p, send_p, far_p, far_out,
-                       sends, recvs, far_recvs, *, tq):
-    p, steps = pl.program_id(0), pl.num_programs(0)
+def attend_back_kernel(len_ref, q_ref, k_ref, v_ref, do_ref, wide_ref, lse_ref, normed_ref, pin_ref, pout_ref, pproj_ref, hin_ref, hout_ref, half_ref,
+                       dqkv_ref, din_ref, dout_ref, dproj_ref, sum_ref, rest_ref,
+                       own_m, got_m, near_m, diag_m, send_m, far_in, far_out, own_p, got_p, near_p, diag_p, send_p, far_p,
+                       parts_s, got_q, near_q, diag_q, send_q, far_q, sends, recvs, far_recvs, far_recvs_q, save_sem, *, tq):
+    p, steps = pl.program_id(0), ATTEND_STEPS
     at = Place()
     G, M = at.G, at.M
     parts = q_ref.shape[0] // tq
+    R = sum_ref.shape[1]
     units = []
 
-    def add(part, bufs, far, total, n, way, kind):
+    def add(part, bufs, far, total, n, way, recv, local=True):
         k = len(units)
-        units.append(SumUnit(at, part, *bufs, far, total, n, way, sends.at[k], recvs.at[k], far_recvs.at[kind], local=True))
+        units.append(SumUnit(at, part, *bufs, far, total, n, way, sends.at[k], recvs.at[k], recv, local=local))
         return units[-1]
 
-    main = []
-    for n in reversed(range(1, M)):
-        main.append([
-            add(lambda c, n=n, ref=ref: ref.at[n - 1, pl.ds(c * G, G)], [b.at[2 * (n - 1) + a] for b in (own_m, got_m, near_m, diag_m, send_m)],
-                far, total, n, a, a)
-            for a, (ref, far, total) in enumerate(((pin_ref, far_in, din_ref), (pout_ref, far_out, dout_ref)))
-        ])
-    proj = [
-        add(lambda c, n=n: pproj_ref.at[at.near[n], c], [b.at[n] for b in (own_p, got_p, near_p, diag_p, send_p)], far_p, dproj_ref, n, n % 2, 2)
-        for n in reversed(range(M))
-    ]
+    def block(n):
+        made = []
+        for a, (ref, far, total) in enumerate(((pin_ref, far_in, din_ref), (pout_ref, far_out, dout_ref))):
+            k = 2 * (n - 1) + a
+            near, diag, out = [b.at[k] for b in (near_m, diag_m, send_m)]
+            own, got = (None, half_ref.at[a]) if n == 1 else (own_m.at[k - 2], got_m.at[k - 2])
+            made.append(add(lambda c, ref=ref: ref.at[n - 2, pl.ds(c * G, G)], (own, got, near, diag, out), far, total, n, a, far_recvs.at[a]))
+        return made
+
+    main = {n: block(n) for n in range(1, M)}
+    for a in range(2):
+        link([main[n][a] for n in main])
+    proj = {}
+    for n in reversed(range(M)):
+        proj[n] = add(lambda c, n=n: pproj_ref.at[at.near[n], c], [b.at[n] for b in (own_p, got_p, near_p, diag_p, send_p)],
+                      far_p, dproj_ref, n, n % 2, far_recvs.at[2])
+    heads = []
+    for t in range(steps // 2 - 1):
+        heads.append({})
+        for n in reversed(range(M)):
+            heads[t][n] = add(lambda c, t=t, n=n: parts_s.at[t, at.near[n], c], [None] + [b.at[t * M + n] for b in (got_q, near_q, diag_q, send_q)],
+                              far_q.at[pl.ds(t * M, M)], sum_ref.at[t], n, (n + t) % 2, far_recvs_q.at[t], False)
+    for group in [proj] + heads:
+        link(list(group.values()))
+    every = lambda group: list(group.values())
+    early = lambda group: [group[n] for n in group if n != 2]
+    late = lambda group: [group[n] for n in group if n == 2]
     plan = {}
 
     def put(slot, name, group):
-        plan.setdefault(min(slot, ATTEND_STEPS * parts - 1), []).extend(getattr(u, name) for u in group)
+        slot = slot + 1 if slot % parts == 0 else slot
+        plan.setdefault(min(slot, steps * parts - 1), []).extend(getattr(u, name) for u in group)
 
     def begin():
         din_ref[...], dout_ref[...] = hin_ref[...], hout_ref[...]
 
-    plan[0] = [at.greet, begin, at.meet]
-    for group in main + [proj]:
-        put(0, "start", group)
-    for n, group in enumerate(main):
-        put(1 + n, "pair", group)
-        put(4 + 2 * n, "cross", group)
-        put(10 + 3 * n, "join", group)
-    put(5, "pair", proj)
-    put(11, "cross", proj)
-    put(18, "join", proj)
-    for group in main + [proj]:
-        put(23, "close", group)
-    attend_back_step(p, len_ref, q_ref, k_ref, v_ref, do_ref, wide_ref, lse_ref, dqkv_ref.at[0], dqkv_ref.at[1], dqkv_ref.at[2], tq, at_slots(p, parts, plan))
+    plan[0] = [at.greet, begin]
+    plan[1] = [at.meet]
+    put(1, "launch", main[1])
+    others = [main[n] for n in reversed(range(2, M))]
+    for group in others + [every(proj)]:
+        put(1, "start", group)
+    for n, group in enumerate(others):
+        put(5 + n, "pair", group)
+        put(13 + 4 * n, "join", group)
+    put(7, "pair", every(proj))
+    put(7, "join", main[1])
+    for group in others[1:]:
+        put(9, "cross", group)
+    put(10, "pair", every(heads[0]))
+    put(11, "cross", every(proj))
+    put(17, "cross", every(heads[0]))
+    put(18, "pair", every(heads[1]))
+    put(19, "join", early(proj))
+    put(21, "cross", every(heads[1]))
+    put(21, "join", late(proj))
+    put(21, "join", early(heads[0]))
+    put(23, "join", late(heads[0]))
+    grad_to = lambda t: dqkv_ref.at[0, :, pl.ds(pl.multiple_of(t * 256 + lax.rem(p, 2) * 128, 128), 128)]
+    attend_back_step(p, len_ref, q_ref, k_ref, v_ref, do_ref, wide_ref, lse_ref, grad_to(0), grad_to(1), grad_to(2), tq, at_slots(p, parts, plan))
+
+    @pl.when(p == 1)
+    def _():
+        for u in others[0]:
+            u.cross()
 
     @pl.when(p == steps - 1)
     def _():
-        for u in units:
-            u.finish()
-
-
-def attend_back(lengths, packed, do, wide, lse, p_in, p_out, p_proj, h_in, h_out, tq):
-    G, M = lax.axis_size("dp") // 2, lax.axis_size("mp")
-    L, D = do.shape
-    pairs = D // 128
-    column = lambda off: pl.BlockSpec((L, 128), lambda p, off=off: (0, off + p))
-    whole = lambda shape: pl.BlockSpec(shape, lambda p: (0,) * len(shape))
-    mshape, pshape = h_in.shape, p_proj.shape[3:]
-    rest = 2 * (M - 1)
-    sems = (rest + M, SumUnit.count(G))
-    return pl.pallas_call(
-        functools.partial(attend_back_kernel, tq=tq),
-        grid=(pairs,),
-        in_specs=[SMEM, column(0), column(pairs), column(2 * pairs), column(0), column(0), whole((L, 128)), ANY, ANY, ANY,
-                  whole(mshape), whole(mshape)],
-        out_specs=[pl.BlockSpec((3, L, 128), lambda p: (0, 0, p)), whole(mshape), whole(mshape), whole(pshape)],
-        out_shape=[jax.ShapeDtypeStruct((3, L, D), BF)]
-        + [jax.ShapeDtypeStruct(mshape, F32)] * 2 + [jax.ShapeDtypeStruct(pshape, F32)],
-        scratch_shapes=sum_buffers(rest, G, mshape, far=M) + sum_buffers(M, G, pshape, far=M)
-        + [pltpu.VMEM((M,) + mshape, BF), DMA(sems), DMA(sems), DMA((3, M))],
-        compiler_params=params_of(2, grid=1),
-    )(lengths, packed, packed, packed, do, wide, lse, p_in, p_out, p_proj, h_in, h_out)
-
-
-def exit_kernel(x_ref, normed_ref, dqkv_ref, w_ref, mid_ref, second_ref, params_ref, grad_ref, qkv_ref, norms_ref,
-                parts_s, got_s, near_s, diag_s, send_s, far_s, norm_s, small_parts, small_got,
-                sends, recvs, far_recvs, small_sends, small_recvs, *, rows):
-    at = Place(everyone=True)
-    G, M = at.G, at.M
-    L, D = x_ref.shape
-    R = qkv_ref.shape[0]
-    small = SmallScatter(at, small_parts, small_got, small_sends, small_recvs)
-    units = []
-    for t in range(3):
-        units.append([
-            SumUnit(at, lambda c, t=t, n=n: parts_s.at[t, at.near[n], c], None, *[b.at[t * M + n] for b in (got_s, near_s, diag_s, send_s)],
-                    far_s.at[pl.ds(t * M, M)], qkv_ref.at[:, pl.ds(t * D, D)], n, (n + t) % 2, sends.at[t * M + n], recvs.at[t * M + n], far_recvs.at[t])
-            for n in reversed(range(M))
-        ])
-
-    def run(t, name):
-        for u in units[t]:
-            getattr(u, name)()
-
-    gain = params_ref[0:1, :]
-    n_norm = L // rows
-    norm_plan = {0: [(1, "cross")], 1: [(2, "pair"), (0, "join")], 2: [(2, "cross")], 3: [(1, "join")]}
-    third_plan = {0: [], 1: [(0, "pair")], 2: [(0, "cross"), (1, "pair")]}
-
-    def third(t, carry):
-        grad = dot(normed_ref[...], dqkv_ref[t], TN)
+        for u in early(heads[1]):
+            u.join()
+
+    @pl.when(lax.rem(p, 2) == 1)
+    def _():
+        t = p // 2
+        grad = dot(normed_ref[...], dqkv_ref[0], TN)
         for g in range(G):
             for c in range(2):
                 for z in range(M):
                     k = ((g * 2 + c) * M + z) * R
                     parts_s[t, z, c, g] = grad[k : k + R, :].astype(BF)
-        for i, items in third_plan.items():
-
-            @pl.when(t == i)
-            def _(i=i, items=items):
-                if i == 0:
+
+    save = pltpu.make_async_copy(parts_s.at[steps // 2 - 1], rest_ref, save_sem.at[0])
+    for t, group in enumerate(heads):
+
+        @pl.when(p == 2 * t + 1)
+        def _(group=group):
+            for u in every(group):
+                u.start()
+
+    @pl.when(p == steps - 1)
+    def _():
+        save.start()
+        for u in late(heads[1]):
+            u.join()
+        for u in units:
+            u.close()
+        for u in units:
+            u.finish(u not in main[1], True)
+        save.wait()
+
+
+def attend_back(lengths, packed, do, wide, lse, normed, p_in, p_out, p_proj, h_in, h_out, halfway, tq):
+    G, M = lax.axis_size("dp") // 2, lax.axis_size("mp")
+    L, D = do.shape
+    pairs = D // 128
+    column = lambda off: pl.BlockSpec((L, 128), lambda p, off=off: (0, off + p))
+    whole = lambda shape: pl.BlockSpec(shape, lambda p: (0,) * len(shape), pipeline_mode=pl.Buffered(1))
+    out = lambda shape: pl.BlockSpec(shape, lambda p: (0,) * len(shape))
+    mshape, pshape = h_in.shape, p_proj.shape[3:]
+    groups = pairs // 2
+    rest = 2 * (M - 1)
+    sems = (rest + groups * M, SumUnit.count(G))
+    return pl.pallas_call(
+        functools.partial(attend_back_kernel, tq=tq),
+        grid=(pairs,),
+        in_specs=[SMEM, column(0), column(pairs), column(2 * pairs), column(0), column(0), whole((L, 128)), whole((L, D)), ANY, ANY, ANY,
+                  whole(mshape), whole(mshape), whole(halfway.shape)],
+        out_specs=[pl.BlockSpec((1, L, 768), lambda p: (p // 2, 0, 0)), out(mshape), out(mshape), out(pshape), out((groups - 1,) + pshape), ANY],
+        out_shape=[jax.ShapeDtypeStruct((groups, L, 768), BF)]
+        + [jax.ShapeDtypeStruct(mshape, F32)] * 2
+        + [jax.ShapeDtypeStruct(pshape, F32), jax.ShapeDtypeStruct((groups - 1,) + pshape, F32), jax.ShapeDtypeStruct((M, 2, G) + pshape, BF)],
+        scratch_shapes=sum_buffers(rest - 2, G, mshape)[:2] + sum_buffers(rest, G, mshape, far=M)[2:] + [pltpu.VMEM((M,) + mshape, BF)] + sum_buffers(M, G, pshape, far=M)
+        + [pltpu.VMEM((groups, M, 2, G) + pshape, BF)] + sum_buffers((groups - 1) * M, G, pshape, own=False, far=(groups - 1) * M)
+        + [DMA(sems), DMA(sems), DMA((3, M)), DMA((groups - 1, M)), DMA((1,))],
+        compiler_params=params_of(2, grid=1),
+    )(lengths, packed, packed, packed, do, wide, lse, normed, p_in, p_out, p_proj, h_in, h_out, halfway)
+
+
+def exit_kernel(x_ref, dqkv_ref, w_ref, mid_ref, second_ref, params_ref, parts_ref, sums_ref, grad_ref, qkv_ref, norms_ref,
+                got_s, near_s, diag_s, send_s, far_s, sum_s, norm_s, e_s, small_parts, small_got,
+                sends, recvs, far_recvs, small_sends, small_recvs, *, rows):
+    at = Place(everyone=True)
+    M = at.M
+    L, D = x_ref.shape
+    R = qkv_ref.shape[0]
+    groups = dqkv_ref.shape[0]
+    small = SmallScatter(at, small_parts, small_got, small_sends, small_recvs)
+    units = [
+        SumUnit(at, lambda c, n=n: parts_ref.at[at.near[n], c], None, *[b.at[n] for b in (got_s, near_s, diag_s, send_s)], far_s, sum_s, n, n % 2,
+                sends.at[n], recvs.at[n], far_recvs)
+        for n in reversed(range(M))
+    ]
+    link(units)
+
+    def run(name, ns=tuple(range(8))):
+        for u in units:
+            if u.n in ns or u.n > 7:
+                getattr(u, name)()
+
+    gain = params_ref[0:1, :]
+    plan = {0: "start", 1: "pair", 2: "cross"}
+
+    def matmul(g, carry):
+        lane = pl.multiple_of(g * 256, 256)
+
+        def piece(i, carry):
+            sl = pl.ds(pl.multiple_of(i * (L // 2), L // 2), L // 2)
+            e = sum(dot(dqkv_ref[g, sl, t * 256 : t * 256 + 256], w_ref[t, :, pl.ds(lane, 256)], NT) for t in range(3))
+            e_s[sl, :] = e_s[sl, :] + e
+            return carry
+
+        lax.fori_loop(0, 2, piece, 0)
+        for j, name in plan.items():
+
+            @pl.when(g == j)
+            def _(j=j, name=name):
+                if j == 0:
                     at.meet()
-                run(i, "start")
-                for item in items:
-                    run(*item)
+                run(name)
 
         return carry
 
     def norm(i, carry):
         sl = pl.ds(pl.multiple_of(i * rows, rows), rows)
-        e = sum(dot(dqkv_ref[t, sl, :], w_ref[t], NT) for t in range(3))
+        e = e_s[sl, :]
         xhat, r = norm_stats(x_ref[sl, :].astype(F32))
         grad_ref[sl, :] = mid_ref[sl, :] + norm_pull(e, xhat, r, gain)
         norm_s[0:1, :] += jnp.sum(e * xhat, axis=0, keepdims=True)
         norm_s[2:3, :] += jnp.sum(e, axis=0, keepdims=True)
-        for j, items in norm_plan.items():
-            if j < n_norm:
-
-                @pl.when(i == j)
-                def _(items=items):
-                    for item in items:
-                        run(*item)
-
         return carry
 
     at.greet()
     norm_s[...] = second_ref[...]
-    lax.fori_loop(0, 3, third, 0)
-    lax.fori_loop(0, n_norm, norm, 0)
+    e_s[...] = jnp.zeros_like(e_s)
+    lax.fori_loop(0, groups, matmul, 0)
+    lax.fori_loop(0, L // rows, norm, 0)
     small.start(norm_s[...], R)
-    for j, items in norm_plan.items():
-        if j >= n_norm:
-            for item in items:
-                run(*item)
-    run(2, "join")
-    run(0, "close")
-    run(1, "close")
+    run("join", (0, 1, 3, 4, 5, 6, 7))
+    for g in range(groups - 1):
+        for t in range(3):
+            qkv_ref[:, pl.ds(t * D + g * 256, 256)] = sums_ref[g, :, pl.ds(t * 256, 256)]
+    run("join", (2,))
     norms_ref[...] = small.collect()
-    run(2, "close")
+    run("close")
     for t in range(3):
-        run(t, "finish")
+        qkv_ref[:, pl.ds(t * D + (groups - 1) * 256, 256)] = sum_s[:, pl.ds(t * 256, 256)]
+    run("finish")
     small.finish()
 
 
-def leave(x, normed, dqkv, w, middle_grad, second_sums, params, R):
+def leave(x, dqkv, w, middle_grad, second_sums, params, parts, sums):
     G, M = lax.axis_size("dp") // 2, lax.axis_size("mp")
     L, D = x.shape
+    R = parts.shape[3]
     n = 2 * G * M
-    sems = (3 * M, SumUnit.count(G))
+    sems = (M, SumUnit.count(G))
     return pl.pallas_call(
         functools.partial(exit_kernel, rows=min(256, L)),
-        in_specs=[VMEM] * 7,
+        in_specs=[VMEM] * 8,
         out_specs=[VMEM] * 3,
         out_shape=[
             jax.ShapeDtypeStruct((L, D), F32),
             jax.ShapeDtypeStruct((R, 3 * D), F32),
             jax.ShapeDtypeStruct((8, 128), F32),
         ],
-        scratch_shapes=[pltpu.VMEM((3, M, 2, G, R, D), BF)] + sum_buffers(3 * M, G, (R, D), own=False, far=3 * M)
-        + [pltpu.VMEM((8, D), F32), pltpu.VMEM((n, 8, 128), F32), pltpu.VMEM((n, 8, 128), F32),
-           DMA(sems), DMA(sems), DMA((3, M)), DMA((n,)), DMA((n,))],
+        scratch_shapes=sum_buffers(M, G, (R, D), own=False, far=M)
+        + [pltpu.VMEM((R, D), F32), pltpu.VMEM((8, D), F32), pltpu.VMEM((L, D), F32), pltpu.VMEM((n, 8, 128), F32), pltpu.VMEM((n, 8, 128), F32),
+           DMA(sems), DMA(sems), DMA((M,)), DMA((n,)), DMA((n,))],
         compiler_params=params_of(3),
-    )(x, normed, dqkv, w, middle_grad, second_sums, params)
+    )(x, dqkv, w, middle_grad, second_sums, params, parts, sums)
 
 
 def per_device(inputs, lengths, attn_qkv, attn_proj, mlp_in, mlp_out, norm_gain, norm_bias, cotangent):
@@ -1015,20 +1093,18 @@
     G = n_dp // 2
     L, D = inputs.shape
     R = attn_qkv.shape[1]
-    here = (lax.axis_index("dp") * n_mp + lax.axis_index("mp")) * R
     small = jnp.concatenate([norm_gain[0], norm_bias[0]], axis=0).astype(F32)
-    placed = lax.dynamic_update_slice(jnp.zeros((8, D), F32), small, (0, here))
     shard = attn_qkv[0].reshape(R, 3, D).transpose(1, 0, 2)
-    wqkv, normed, params = entry(inputs, shard, placed)
+    wqkv, normed, params = entry(inputs, shard, jnp.pad(small, ((0, 4), (0, 128 - R))))
     wqkv = wqkv.reshape(3, D, D)
     io = jnp.stack([mlp_in[0], mlp_out[0].T])
     mixed, wide, lse, packed, wproj, land, win, wout = attend(lengths, normed, wqkv, attn_proj[0], io, min(512, L))
     pieces = lambda w: w.reshape((w.shape[0], n_dp) + w.shape[3:])
-    outputs, middle_grad, mixed_grad, second_sums, p_proj, p_in, p_out, h_in, h_out = mlp(
+    outputs, middle_grad, mixed_grad, second_sums, p_proj, p_in, p_out, h_in, h_out, halfway = mlp(
         lengths, inputs, mixed, cotangent, params, wproj.reshape(D, D), pieces(win), pieces(wout), land, R, min(512, L))
-    dqkv, d_in, d_out, d_proj = attend_back(
-        lengths, packed, mixed_grad, wide, lse, p_in, p_out, p_proj, h_in, h_out, min(256, L))
-    input_grad, d_qkv, norms = leave(inputs, normed, dqkv, wqkv, middle_grad, second_sums, params, R)
+    dqkv, d_in, d_out, d_proj, sums, parts = attend_back(
+        lengths, packed, mixed_grad, wide, lse, normed, p_in, p_out, p_proj, h_in, h_out, halfway, min(256, L))
+    input_grad, d_qkv, norms = leave(inputs, dqkv, wqkv, middle_grad, second_sums, params, parts, sums)
     return (
         outputs,
         input_grad,

time: 252 us -> 241 us (0.956)
  Pallas kernels: 239 us -> 227 us
    pallas_call x1, Pallas kernels: 39.4 us -> 28 us  [leave(): pl.pallas_call(functools.partial(exit_kernel, rows=min(256, L)), in_specs...]
    pallas_call x1, Pallas kernels: 51.3 us -> 43 us  [attend(): pl.pallas_call(functools.partial(attend_kernel, tq=tq), grid=(D // 128,),...]
    pallas_call x1, Pallas kernels: 57.9 us -> 64.5 us  [attend_back(): pl.pallas_call(functools.partial(attend_back_kernel, tq=tq), grid=(pairs,...]
    unnamed x20 -> x18, local copies, waits for them, and re-layouts: 5.59 us -> 6.89 us
where the time goes in v1:
time: 241 us
  Pallas kernels  227 us (94%)
  local copies, waits for them, and re-layouts  9.81 us (4%)
  other arithmetic  3 us (1%)
    pallas_call x1, Pallas kernels, attend_back(): pl.pallas_call(functools.partial(attend_back_kernel, tq=tq), grid=(pairs,...  64.5 us
    pallas_call x1, Pallas kernels, mlp(): pl.pallas_call(functools.partial(mlp_kernel, tr=tr), in_specs=[SMEM, VMEM...  55.4 us
    pallas_call x1, Pallas kernels, attend(): pl.pallas_call(functools.partial(attend_kernel, tq=tq), grid=(D // 128,),...  43 us
    pallas_call x1, Pallas kernels, entry(): pl.pallas_call(functools.partial(entry_kernel, rows=min(256, L)), in_spec...  35.7 us
    pallas_call x1, Pallas kernels, leave(): pl.pallas_call(functools.partial(exit_kernel, rows=min(256, L)), in_specs...  28 us
    unnamed x18, local copies, waits for them, and re-layouts  6.89 us

profile of v1, /device:TPU:0, one launch (start us, length us, event | category | flops | bytes accessed | tf_op | source)
XLA Modules:
  0.0 240.7 jit_solution(7071604798063545149)
XLA Ops:
  1.3 1.3 fusion.6.own_ref
  2.6 0.9 reshape_squeeze.3
  3.5 0.7 copy.19
  4.2 1.7 pad_maximum_fusion.io_ref
  5.9 35.7 %shard_map.152 = (bf16[3,4,2,4,24,768]{5,4,3,2,1,0:T(8,128)(2,1)}, bf16[1024,768]{1,0:T(8,128)(2,1)}, f32[8,768]{1,0:T(8,128)}) custom-call(bf16[1024,768]{1,0:T(8,128)(2,1)} %x_ref.5, bf16[3,24,768]{2,1,0:T(8,128)(2,1)} %bitcast.30, f32[8,128]{1,0:T(8,128)} %fusion.6.own_ref), custom_call_target="tpu_custom_call" | custom-call | tf_op jit(solution)/shard_map/pallas_call | solution.py:420
  41.6 43.0 %shard_map.153 = (bf16[1024,768]{1,0:T(8,128)(2,1)}, f32[1024,768]{1,0:T(8,128)}, f32[1024,128]{1,0:T(8,128)}, bf16[1024,2304]{1,0:T(8,128)(2,1)}, bf16[4,2,4,24...) custom-call(s32[1]{0:T(128)S(6)} %copy.26.len_ref, ...), custom_call_target="tpu_custom_call" | custom-call | tf_op jit(solution)/shard_map/pallas_call | solution.py:653
  84.6 55.4 %shard_map.154 = (bf16[1024,768]{1,0:T(8,128)(2,1)}, f32[1024,768]{1,0:T(8,128)}, bf16[1024,768]{1,0:T(8,128)(2,1)}, f32[8,768]{1,0:T(8,128)}, bf16[4,2,4,24,768...) custom-call(s32[1]{0:T(128)S(6)} %copy.26.len_ref, ...), custom_call_target="tpu_custom_call" | custom-call | tf_op jit(solution)/shard_map/pallas_call | solution.py:831
  140.0 64.5 %shard_map.155 = (bf16[3,1024,768]{2,1,0:T(8,128)(2,1)}, f32[96,768]{1,0:T(8,128)}, f32[96,768]{1,0:T(8,128)}, f32[24,768]{1,0:T(8,128)}, f32[2,24,768]{2,1,0:T(8,128)}, /*index=5*/bf16[4,2,4,24,768]{4,3,2,1,0:T(8,128)(2,1)}) custom-call(s32[1]{0:T(128)S(6)} %copy.26.len_ref, bf16[1024,2304]{1,0:T(8,128)(2,1)} %get-tuple-element.47.q_ref.k_ref.v_ref, ...), custom_call_target="tpu_custom_call" | custom-call | tf_op jit(solution)/shard_map/pallas_call | solution.py:981
  204.5 0.0 copy-start.1
  204.5 28.0 %shard_map.156 = (f32[1024,768]{1,0:T(8,128)}, f32[24,2304]{1,0:T(8,128)}, f32[8,128]{1,0:T(8,128)}) custom-call(bf16[1024,768]{1,0:T(8,128)(2,1)} %x_ref.5, bf16[3,1024,768]{2,1,0:T(8,128)(2,1)} %get-tuple-element.57.dqkv_ref, bf16[3,768,768]{2,1,0:T(8,128)(2,1)} %bitcast.26, f32[1024,768]{1,0:T(8,128)} %get-tuple-element.58.mid_ref, ...), custom_call_target="tpu_custom_call" | custom-call | tf_op jit(solution)/shard_map/pallas_call | solution.py:1075
  232.5 1.3 slice_bitcast_fusion
  233.8 0.0 copy-done.1
  233.8 0.0 copy-start
  233.8 1.1 copy.27
  235.0 1.3 copy-done
  236.3 0.0 copy-start.4
  236.3 0.0 copy-start.5
  236.3 0.0 copy-start.3
  236.3 0.0 copy-start.2
  236.3 1.7 copy.28
  238.0 0.0 copy-done.4
  238.0 0.7 copy.29
  238.7 0.0 copy-done.5
  238.7 0.6 copy.30
  239.3 0.0 copy-done.3
  239.3 0.7 copy.31
  240.0 0.0 copy-done.2
  240.0 0.7 copy.32
Async XLA Ops:
  204.5 29.3 %copy-start.1 = (bf16[1024,768]{1,0:T(8,128)(2,1)S(1)}, bf16[1024,768]{1,0:T(8,128)(2,1)}, u32[]{:S(2)}) copy-start(bf16[1024,768]{1,0:T(8,128)(2,1)} %get-tuple-element.78) | copy-start | bytes 4718596
  233.8 2.5 %copy-start = (f32[1024,768]{1,0:T(8,128)S(1)}, f32[1024,768]{1,0:T(8,128)}, u32[]{:S(2)}) copy-start(f32[1024,768]{1,0:T(8,128)} %get-tuple-element.79) | copy-start | bytes 9437188
  236.3 1.7 copy-start.4
  236.3 2.4 copy-start.5
  236.3 3.0 %copy-start.3 = (f32[96,768]{1,0:T(8,128)S(1)}, f32[96,768]{1,0:T(8,128)}, u32[]{:S(2)}) copy-start(f32[96,768]{1,0:T(8,128)} %get-tuple-element.65) | copy-start | bytes 884740
  236.3 3.7 %copy-start.2 = (f32[96,768]{1,0:T(8,128)S(1)}, f32[96,768]{1,0:T(8,128)}, u32[]{:S(2)}) copy-start(f32[96,768]{1,0:T(8,128)} %get-tuple-element.66) | copy-start | bytes 884740

commit v2 on v1

--- a/solution.py
+++ b/solution.py
@@ -368,7 +368,7 @@
     return r * (y - jnp.mean(y, axis=-1, keepdims=True) - xhat * jnp.mean(y * xhat, axis=-1, keepdims=True))
 
 
-def entry_kernel(x_ref, shard_ref, own_ref, w_ref, normed_ref, params_ref, got, chain_sends, chain_recvs, sends, recvs,
+def entry_kernel(x_ref, block_ref, gain_ref, bias_ref, w_ref, normed_ref, params_ref, shard_ref, own_ref, got, chain_sends, chain_recvs, sends, recvs,
                  small_sends, small_recvs, *, rows):
     at = Place(everyone=True)
     at.greet()
@@ -380,6 +380,12 @@
     ]
     small = SmallGather(at, got, small_sends, small_recvs)
     L, D = x_ref.shape
+    R = block_ref.shape[0]
+    for t in range(3):
+        shard_ref[t] = block_ref[:, pl.ds(t * D, D)]
+    own_ref[...] = jnp.zeros_like(own_ref)
+    own_ref[0:2, 0:R] = gain_ref[...].astype(F32)
+    own_ref[2:4, 0:R] = bias_ref[...].astype(F32)
     at.meet()
     chain.start(1)
     units[0].spread()
@@ -399,7 +405,7 @@
         units[n - 1].relay()
         if n > 1:
             units[n - 2].last()
-    params_ref[...] = small.collect(own_ref, shard_ref.shape[1], D)
+    params_ref[...] = small.collect(own_ref, R, D)
     lax.fori_loop(0, steps // 2, norm, 0)
     units[-1].relay()
     if at.M > 1:
@@ -412,23 +418,24 @@
     small.finish(own_ref)
 
 
-def entry(x, shard, own):
+def entry(x, block, gain, bias):
     G, M = lax.axis_size("dp") // 2, lax.axis_size("mp")
     L, D = x.shape
+    R = block.shape[0]
     n = 2 * G * M
     sems = (M, GatherUnit.count(G))
     return pl.pallas_call(
         functools.partial(entry_kernel, rows=min(256, L)),
-        in_specs=[VMEM, ANY, VMEM],
+        in_specs=[VMEM] * 4,
         out_specs=[ANY, VMEM, VMEM],
         out_shape=[
-            jax.ShapeDtypeStruct((3, G, 2, M) + shard.shape[1:], BF),
+            jax.ShapeDtypeStruct((3, G, 2, M, R, D), BF),
             jax.ShapeDtypeStruct((L, D), BF),
             jax.ShapeDtypeStruct((8, D), F32),
         ],
-        scratch_shapes=[pltpu.VMEM((n,) + own.shape, F32), DMA((M + 1,)), DMA((M,)), DMA(sems), DMA(sems), DMA((n,)), DMA((n,))],
+        scratch_shapes=[pltpu.VMEM((3, R, D), BF), pltpu.VMEM((8, 128), F32), pltpu.VMEM((n, 8, 128), F32), DMA((M + 1,)), DMA((M,)), DMA(sems), DMA(sems), DMA((n,)), DMA((n,))],
         compiler_params=params_of(0),
-    )(x, shard, own)
+    )(x, block, gain, bias)
 
 
 def lanes(shape):
@@ -546,7 +553,7 @@
     return between
 
 
-def attend_kernel(len_ref, x_ref, w_ref, proj_ref, io_ref, o_ref, wide_ref, lse_ref, packed_ref, wproj_ref, land_ref, win_ref, wout_ref,
+def attend_kernel(len_ref, x_ref, w_ref, proj_ref, in_ref, out_ref, o_ref, wide_ref, lse_ref, packed_ref, wproj_ref, land_ref, win_ref, wout_ref,
                   packed_s, save_sem, pchain_sends, pchain_recvs, chain_sends, chain_recvs, sends, recvs, *, tq):
     p, steps = pl.program_id(0), pl.num_programs(0)
     at = Place()
@@ -555,11 +562,12 @@
     D = x_ref.shape[1]
     parts = x_ref.shape[0] // tq
     land = [lambda s, a=a: land_ref.at[s, a] for a in range(2)]
+    own = (in_ref, out_ref)
     pland = lambda s: wproj_ref.at[at.g, at.c, s]
     pchain = Along(at, proj_ref, pland, pchain_sends, pchain_recvs)
-    chains = [Along(at, io_ref.at[a], land[a], chain_sends.at[a], chain_recvs.at[a]) for a in range(2)]
+    chains = [Along(at, own[a], land[a], chain_sends.at[a], chain_recvs.at[a]) for a in range(2)]
     main = [
-        [GatherUnit(at, land[a](at.near[n]) if n else io_ref.at[a], lambda g, c, n=n, ref=ref: ref.at[n, g, c], a, sends.at[2 * n + a], recvs.at[2 * n + a])
+        [GatherUnit(at, land[a](at.near[n]) if n else own[a], lambda g, c, n=n, ref=ref: ref.at[n, g, c], a, sends.at[2 * n + a], recvs.at[2 * n + a])
          for a, ref in enumerate((win_ref, wout_ref))]
         for n in range(half)
     ]
@@ -568,7 +576,7 @@
                    sends.at[2 * half + n], recvs.at[2 * half + n], n == 0)
         for n in range(M)
     ]
-    own_land = [pltpu.make_async_copy(io_ref.at[a], land_ref.at[at.z, a], save_sem.at[1 + a]) for a in range(2)]
+    own_land = [pltpu.make_async_copy(own[a], land_ref.at[at.z, a], save_sem.at[1 + a]) for a in range(2)]
     save = pltpu.make_async_copy(packed_s, packed_ref, save_sem.at[0])
 
     def third(t):
@@ -605,23 +613,19 @@
 
         return act
 
-    for n in range(1, M):
-        put((1, 4, 6)[min(n, 3) - 1], arrive(pchain, n, proj[n]))
-    put(2, proj[0].relay)
-    for n in range(1, half):
-        put(1 + 2 * n, arrive(chains[0], n, main[n][0]))
-        put(2 + 2 * n, arrive(chains[1], n, main[n][1]))
-    put(4, main[0][0].relay, main[0][1].relay)
-    put(5, proj[0].last)
-    for n in range(1, M):
-        put(3 + 2 * n, proj[n].relay)
-        put(min(6 + 2 * n, 11), proj[n].last)
-    for n in range(1, half):
-        put(6 + n, main[n][0].relay)
-        put(7 + n, main[n][1].relay)
-    put(8, main[0][0].last, main[0][1].last)
-    for n in range(1, half):
-        put(10 + n, main[n][0].last, main[n][1].last)
+    for n in range(M):
+        arrives, relays, lasts = ATTEND_PROJ[min(n, 3)]
+        put(relays, proj[n].relay)
+        put(lasts, proj[n].last)
+        if n:
+            put(arrives, arrive(pchain, n, proj[n]))
+    for n in range(half):
+        for a in range(2):
+            arrives, relays, lasts = ATTEND_MAIN[min(n, 1)][a]
+            if n:
+                put(arrives, arrive(chains[a], n, main[n][a]))
+            put(relays, main[n][a].relay)
+            put(lasts, main[n][a].last)
     lane = pl.multiple_of(p * 128, 128)
     column = lambda t: packed_s.at[:, pl.ds(t * D + lane, 128)]
     attend_step(p, len_ref, column(0), column(1), column(2), o_ref, wide_ref, lse_ref, tq, at_slots(p, parts, plan))
@@ -640,20 +644,25 @@
 
 
 ATTEND_STEPS = 6
-
-
-def attend(lengths, x, w, proj, io, tq):
+ATTEND_PROJ = [[0, 2, 5], [1, 5, 8], [4, 7, 10], [6, 9, 11]]
+ATTEND_MAIN = [[[0, 4, 8], [0, 4, 8]], [[3, 7, 11], [4, 8, 11]]]
+BACK = {"pair0": 5, "pair1": 6, "pair_p": 7, "join_1": 7, "cross1": 9, "pair_h0": 10, "cross_p": 11, "join0": 13, "join1": 17, "cross_h0": 17,
+        "pair_h1": 18, "join_p": 19, "cross_h1": 21, "late_p": 21, "join_h0": 21, "late_h0": 23}
+MLP = {"relay0": (0, 3), "spread1": (0, 3), "relay1": (1, 3), "last0": (1, 2), "last1": (2, 2), "pair0": (1, 2), "cross0": (2, 1), "pair1": (2, 3), "join0": (3, 1)}
+
+
+def attend(lengths, x, w, proj, w_in, w_out, tq):
     G, M = lax.axis_size("dp") // 2, lax.axis_size("mp")
     L, D = x.shape
     half = M // 2
     column = pl.BlockSpec((L, 128), lambda p: (0, p))
     whole = lambda shape: pl.BlockSpec(shape, lambda p: (0,) * len(shape), pipeline_mode=pl.Buffered(1))
     sems = (2 * half + M, GatherUnit.count(G))
-    weights = jax.ShapeDtypeStruct((half, G, 2) + io.shape[1:], BF)
+    weights = jax.ShapeDtypeStruct((half, G, 2) + w_in.shape, BF)
     return pl.pallas_call(
         functools.partial(attend_kernel, tq=tq),
         grid=(D // 128,),
-        in_specs=[SMEM, whole(x.shape), whole(w.shape), ANY, ANY],
+        in_specs=[SMEM, whole(x.shape), whole(w.shape), ANY, ANY, ANY],
         out_specs=[column, column, pl.BlockSpec((L, 128), lambda p: (0, 0)), ANY, ANY, ANY, ANY, ANY],
         out_shape=[
             jax.ShapeDtypeStruct((L, D), BF),
@@ -661,12 +670,12 @@
             jax.ShapeDtypeStruct((L, 128), F32),
             jax.ShapeDtypeStruct((L, 3 * D), BF),
             jax.ShapeDtypeStruct((G, 2, M) + proj.shape, BF),
-            jax.ShapeDtypeStruct((M,) + io.shape, BF),
+            jax.ShapeDtypeStruct((M, 2) + w_in.shape, BF),
             weights, weights,
         ],
         scratch_shapes=[pltpu.VMEM((L, 3 * D), BF), DMA((3,)), DMA((M + 1,)), DMA((M,)), DMA((2, M + 1)), DMA((2, M)), DMA(sems), DMA(sems)],
         compiler_params=params_of(1, grid=1),
-    )(lengths, x, w, proj, io)
+    )(lengths, x, w, proj, w_in, w_out)
 
 
 def gelu_and_slope(x):
@@ -730,19 +739,19 @@
     def put(k, i, name, group):
         plan.setdefault((min(k, M - 1), min(i, per - 1)), []).extend(getattr(u, name) for u in group)
 
-    put(0, 3, "relay", gathers[0])
     for n, group in enumerate(gathers):
+        after = lambda name: (MLP[name + "0"] if n == 0 else (MLP[name + "1"][0] + n - 1, MLP[name + "1"][1]))
+        put(*after("relay"), "relay", group)
         if n:
-            put(0, 3, "spread", group[1:])
-            put(n, 3, "relay", group)
-        put(n + 1, 2, "last", group)
+            put(*MLP["spread1"], "spread", group[1:])
+        put(*after("last"), "last", group)
         put(half + n, 0, "finish", group)
     put(1, 0, "start", sums[0])
-    put(1, 2, "pair", sums[0])
+    put(*MLP["pair0"], "pair", sums[0])
     put(2, 0, "start", sums[1])
-    put(2, 1, "cross", sums[0])
-    plan.setdefault((2, 3), []).extend(functools.partial(u.pair, True) for u in sums[1])
-    put(3, 1, "join", sums[0])
+    put(*MLP["cross0"], "cross", sums[0])
+    plan.setdefault(MLP["pair1"], []).extend(functools.partial(u.pair, True) for u in sums[1])
+    put(*MLP["join0"], "join", sums[0])
 
     def block(k, carry):
         def between(i):
@@ -909,21 +918,21 @@
     for group in others + [every(proj)]:
         put(1, "start", group)
     for n, group in enumerate(others):
-        put(5 + n, "pair", group)
-        put(13 + 4 * n, "join", group)
-    put(7, "pair", every(proj))
-    put(7, "join", main[1])
+        put(BACK["pair0"] if n == 0 else BACK["pair1"], "pair", group)
+        put(BACK["join0"] if n == 0 else BACK["join1"], "join", group)
+    put(BACK["pair_p"], "pair", every(proj))
+    put(BACK["join_1"], "join", main[1])
     for group in others[1:]:
-        put(9, "cross", group)
-    put(10, "pair", every(heads[0]))
-    put(11, "cross", every(proj))
-    put(17, "cross", every(heads[0]))
-    put(18, "pair", every(heads[1]))
-    put(19, "join", early(proj))
-    put(21, "cross", every(heads[1]))
-    put(21, "join", late(proj))
-    put(21, "join", early(heads[0]))
-    put(23, "join", late(heads[0]))
+        put(BACK["cross1"], "cross", group)
+    put(BACK["pair_h0"], "pair", every(heads[0]))
+    put(BACK["cross_p"], "cross", every(proj))
+    put(BACK["cross_h0"], "cross", every(heads[0]))
+    put(BACK["pair_h1"], "pair", every(heads[1]))
+    put(BACK["join_p"], "join", early(proj))
+    put(BACK["cross_h1"], "cross", every(heads[1]))
+    put(BACK["late_p"], "join", late(proj))
+    put(BACK["join_h0"], "join", early(heads[0]))
+    put(BACK["late_h0"], "join", late(heads[0]))
     grad_to = lambda t: dqkv_ref.at[0, :, pl.ds(pl.multiple_of(t * 256 + lax.rem(p, 2) * 128, 128), 128)]
     attend_back_step(p, len_ref, q_ref, k_ref, v_ref, do_ref, wide_ref, lse_ref, grad_to(0), grad_to(1), grad_to(2), tq, at_slots(p, parts, plan))
 
@@ -1093,12 +1102,9 @@
     G = n_dp // 2
     L, D = inputs.shape
     R = attn_qkv.shape[1]
-    small = jnp.concatenate([norm_gain[0], norm_bias[0]], axis=0).astype(F32)
-    shard = attn_qkv[0].reshape(R, 3, D).transpose(1, 0, 2)
-    wqkv, normed, params = entry(inputs, shard, jnp.pad(small, ((0, 4), (0, 128 - R))))
+    wqkv, normed, params = entry(inputs, attn_qkv[0], norm_gain[0], norm_bias[0])
     wqkv = wqkv.reshape(3, D, D)
-    io = jnp.stack([mlp_in[0], mlp_out[0].T])
-    mixed, wide, lse, packed, wproj, land, win, wout = attend(lengths, normed, wqkv, attn_proj[0], io, min(512, L))
+    mixed, wide, lse, packed, wproj, land, win, wout = attend(lengths, normed, wqkv, attn_proj[0], mlp_in[0], mlp_out[0].T, min(512, L))
     pieces = lambda w: w.reshape((w.shape[0], n_dp) + w.shape[3:])
     outputs, middle_grad, mixed_grad, second_sums, p_proj, p_in, p_out, h_in, h_out, halfway = mlp(
         lengths, inputs, mixed, cotangent, params, wproj.reshape(D, D), pieces(win), pieces(wout), land, R, min(512, L))

time: 241 us -> 236 us (0.979)
  other arithmetic: 3 us -> 0 us
where the time goes in v2:
time: 236 us
  Pallas kernels  226 us (96%)
  local copies, waits for them, and re-layouts  8.2 us (3%)
    pallas_call x1, Pallas kernels, attend_back(): pl.pallas_call(functools.partial(attend_back_kernel, tq=tq), grid=(pairs,...  64.8 us
    pallas_call x1, Pallas kernels, mlp(): pl.pallas_call(functools.partial(mlp_kernel, tr=tr), in_specs=[SMEM, VMEM...  55.2 us
    pallas_call x1, Pallas kernels, attend(): pl.pallas_call(functools.partial(attend_kernel, tq=tq), grid=(D // 128,),...  42.7 us
    pallas_call x1, Pallas kernels, entry(): pl.pallas_call(functools.partial(entry_kernel, rows=min(256, L)), in_spec...  36.1 us
    pallas_call x1, Pallas kernels, leave(): pl.pallas_call(functools.partial(exit_kernel, rows=min(256, L)), in_specs...  27.2 us
    unnamed x18, local copies, waits for them, and re-layouts  6.89 us

profile of v2, /device:TPU:0, one launch (start us, length us, event | category | flops | bytes accessed | tf_op | source)
XLA Modules:
  0.0 235.6 jit_solution(17390264539815932715)
XLA Ops:
  1.3 36.1 %shard_map.152 = (bf16[3,4,2,4,24,768]{5,4,3,2,1,0:T(8,128)(2,1)}, bf16[1024,768]{1,0:T(8,128)(2,1)}, f32[8,768]{1,0:T(8,128)}) custom-call(bf16[1024,768]{1,0:T(8,128)(2,1)} %x_ref.5, bf16[24,2304]{1,0:T(8,128)(2,1)} %bitcast.32, bf16[2,24]{1,0:T(2,128)(2,1)} %bitcast.35, bf16[2,24]{1,0:T(2,128)(2,1)} %bitcast.36), custom_call_target="tpu_custom_call" | custom-call | tf_op jit(solution)/shard_map/pallas_call | solution.py:427
  37.4 42.7 %shard_map.153 = (bf16[1024,768]{1,0:T(8,128)(2,1)}, f32[1024,768]{1,0:T(8,128)}, f32[1024,128]{1,0:T(8,128)}, bf16[1024,2304]{1,0:T(8,128)(2,1)}, bf16[4,2,4,24...) custom-call(s32[1]{0:T(128)S(6)} %copy.23.len_ref, ...), custom_call_target="tpu_custom_call" | custom-call | tf_op jit(solution)/shard_map/pallas_call | solution.py:662
  80.1 55.2 %shard_map.154 = (bf16[1024,768]{1,0:T(8,128)(2,1)}, f32[1024,768]{1,0:T(8,128)}, bf16[1024,768]{1,0:T(8,128)(2,1)}, f32[8,768]{1,0:T(8,128)}, bf16[4,2,4,24,768...) custom-call(s32[1]{0:T(128)S(6)} %copy.23.len_ref, ...), custom_call_target="tpu_custom_call" | custom-call | tf_op jit(solution)/shard_map/pallas_call | solution.py:840
  135.4 64.8 %shard_map.155 = (bf16[3,1024,768]{2,1,0:T(8,128)(2,1)}, f32[96,768]{1,0:T(8,128)}, f32[96,768]{1,0:T(8,128)}, f32[24,768]{1,0:T(8,128)}, f32[2,24,768]{2,1,0:T(8,128)}, /*index=5*/bf16[4,2,4,24,768]{4,3,2,1,0:T(8,128)(2,1)}) custom-call(s32[1]{0:T(128)S(6)} %copy.23.len_ref, bf16[1024,2304]{1,0:T(8,128)(2,1)} %get-tuple-element.47.q_ref.k_ref.v_ref, ...), custom_call_target="tpu_custom_call" | custom-call | tf_op jit(solution)/shard_map/pallas_call | solution.py:990
  200.2 0.0 copy-start.1
  200.2 27.2 %shard_map.156 = (f32[1024,768]{1,0:T(8,128)}, f32[24,2304]{1,0:T(8,128)}, f32[8,128]{1,0:T(8,128)}) custom-call(bf16[1024,768]{1,0:T(8,128)(2,1)} %x_ref.5, bf16[3,1024,768]{2,1,0:T(8,128)(2,1)} %get-tuple-element.57.dqkv_ref, bf16[3,768,768]{2,1,0:T(8,128)(2,1)} %bitcast.23, f32[1024,768]{1,0:T(8,128)} %get-tuple-element.58.mid_ref, ...), custom_call_target="tpu_custom_call" | custom-call | tf_op jit(solution)/shard_map/pallas_call | solution.py:1084
  227.4 1.3 slice_bitcast_fusion
  228.7 0.0 copy-done.1
  228.7 0.0 copy-start
  228.7 1.1 copy.24
  229.9 1.3 copy-done
  231.2 0.0 copy-start.4
  231.2 0.0 copy-start.5
  231.2 0.0 copy-start.3
  231.2 0.0 copy-start.2
  231.2 1.7 copy.25
  232.8 0.0 copy-done.4
  232.9 0.7 copy.26
  233.5 0.0 copy-done.5
  233.5 0.6 copy.27
  234.2 0.0 copy-done.3
  234.2 0.7 copy.28
  234.9 0.0 copy-done.2
  234.9 0.7 copy.29
Async XLA Ops:
  200.2 28.5 %copy-start.1 = (bf16[1024,768]{1,0:T(8,128)(2,1)S(1)}, bf16[1024,768]{1,0:T(8,128)(2,1)}, u32[]{:S(2)}) copy-start(bf16[1024,768]{1,0:T(8,128)(2,1)} %get-tuple-element.78) | copy-start | bytes 4718596
  228.7 2.5 %copy-start = (f32[1024,768]{1,0:T(8,128)S(1)}, f32[1024,768]{1,0:T(8,128)}, u32[]{:S(2)}) copy-start(f32[1024,768]{1,0:T(8,128)} %get-tuple-element.79) | copy-start | bytes 9437188
  231.2 1.7 copy-start.4
  231.2 2.4 %copy-start.5 = (f32[24,768]{1,0:T(8,128)S(1)}, f32[24,768]{1,0:T(8,128)}, u32[]{:S(2)}) copy-start(f32[24,768]{1,0:T(8,128)} %get-tuple-element.64) | copy-start | bytes 221188
  231.2 3.0 %copy-start.3 = (f32[96,768]{1,0:T(8,128)S(1)}, f32[96,768]{1,0:T(8,128)}, u32[]{:S(2)}) copy-start(f32[96,768]{1,0:T(8,128)} %get-tuple-element.65) | copy-start | bytes 884740
  231.2 3.7 %copy-start.2 = (f32[96,768]{1,0:T(8,128)S(1)}, f32[96,768]{1,0:T(8,128)}, u32[]{:S(2)}) copy-start(f32[96,768]{1,0:T(8,128)} %get-tuple-element.66) | copy-start | bytes 884740

commit v3 on v2

--- a/solution.py
+++ b/solution.py
@@ -96,6 +96,10 @@
         for n in ns:
             self._copy(n, self.at.z).start()
 
+    def pass_on(self):
+        block = self.land(self.at.near[2])
+        remote(block, block, self.sends.at[3], self.recvs.at[self.at.near[2]], self.at.along(self.at.near[1])).start()
+
     def arrive(self, n):
         self._copy(n, self.at.near[n]).wait_recv()
 
@@ -170,7 +174,7 @@
         self.out, self.far, self.total, self.n, self.way = out, far, total, n, way
         self.sends, self.recvs, self.far_recvs, self.local = sends, recvs, far_recvs, local
         self.place = at.near[n]
-        self.passed = at.M == 4 and n == 3
+        self.passed = False
         self.opposite = None
 
     @staticmethod
@@ -274,6 +278,7 @@
     by_n = {u.n: u for u in units}
     if units[0].at.M == 4 and 3 in by_n:
         by_n[2].opposite = by_n[3]
+        by_n[3].passed = True
     return units
 
 
@@ -389,7 +394,7 @@
     at.meet()
     chain.start(1)
     units[0].spread()
-    chain.start(*range(2, at.M))
+    chain.start(*range(2, 3 if at.M == 4 else at.M))
     small.start(own_ref)
 
     def norm(i, carry):
@@ -401,6 +406,8 @@
     steps = L // rows
     for n in range(1, at.M):
         chain.arrive(n)
+        if at.M == 4 and n == 2:
+            chain.pass_on()
         units[n].spread()
         units[n - 1].relay()
         if n > 1:
@@ -554,7 +561,7 @@
 
 
 def attend_kernel(len_ref, x_ref, w_ref, proj_ref, in_ref, out_ref, o_ref, wide_ref, lse_ref, packed_ref, wproj_ref, land_ref, win_ref, wout_ref,
-                  packed_s, save_sem, pchain_sends, pchain_recvs, chain_sends, chain_recvs, sends, recvs, *, tq):
+                  w_s, w_sem, packed_s, save_sem, pchain_sends, pchain_recvs, chain_sends, chain_recvs, sends, recvs, *, tq):
     p, steps = pl.program_id(0), pl.num_programs(0)
     at = Place()
     M = at.M
@@ -579,11 +586,16 @@
     own_land = [pltpu.make_async_copy(own[a], land_ref.at[at.z, a], save_sem.at[1 + a]) for a in range(2)]
     save = pltpu.make_async_copy(packed_s, packed_ref, save_sem.at[0])
 
+    loads = [pltpu.make_async_copy(w_ref.at[t], w_s.at[t], w_sem.at[t]) for t in range(3)]
+
     def third(t):
-        packed_s[:, pl.ds(t * D, D)] = dot(x_ref[...], w_ref[t], NN).astype(BF)
+        loads[t].wait()
+        packed_s[:, pl.ds(t * D, D)] = dot(x_ref[...], w_s[t], NN).astype(BF)
 
     @pl.when(p == 0)
     def _():
+        for cp in loads:
+            cp.start()
         at.greet()
         third(0)
         at.meet()
@@ -646,8 +658,8 @@
 ATTEND_STEPS = 6
 ATTEND_PROJ = [[0, 2, 5], [1, 5, 8], [4, 7, 10], [6, 9, 11]]
 ATTEND_MAIN = [[[0, 4, 8], [0, 4, 8]], [[3, 7, 11], [4, 8, 11]]]
-BACK = {"pair0": 5, "pair1": 6, "pair_p": 7, "join_1": 7, "cross1": 9, "pair_h0": 10, "cross_p": 11, "join0": 13, "join1": 17, "cross_h0": 17,
-        "pair_h1": 18, "join_p": 19, "cross_h1": 21, "late_p": 21, "join_h0": 21, "late_h0": 23}
+BACK = {"pair0": 5, "pair1": 6, "pair_p": 7, "join_1": 7, "cross1": 9, "pair_h0": 10, "cross_p": 11, "join0": 13, "cross_h0": 17,
+        "pair_h1": 17, "join_p": 19, "cross_h1": 19, "late_p": 21, "join_h0": 21, "late_h0": 23, "join_h1": 23}
 MLP = {"relay0": (0, 3), "spread1": (0, 3), "relay1": (1, 3), "last0": (1, 2), "last1": (2, 2), "pair0": (1, 2), "cross0": (2, 1), "pair1": (2, 3), "join0": (3, 1)}
 
 
@@ -662,7 +674,7 @@
     return pl.pallas_call(
         functools.partial(attend_kernel, tq=tq),
         grid=(D // 128,),
-        in_specs=[SMEM, whole(x.shape), whole(w.shape), ANY, ANY, ANY],
+        in_specs=[SMEM, whole(x.shape), ANY, ANY, ANY, ANY],
         out_specs=[column, column, pl.BlockSpec((L, 128), lambda p: (0, 0)), ANY, ANY, ANY, ANY, ANY],
         out_shape=[
             jax.ShapeDtypeStruct((L, D), BF),
@@ -673,7 +685,7 @@
             jax.ShapeDtypeStruct((M, 2) + w_in.shape, BF),
             weights, weights,
         ],
-        scratch_shapes=[pltpu.VMEM((L, 3 * D), BF), DMA((3,)), DMA((M + 1,)), DMA((M,)), DMA((2, M + 1)), DMA((2, M)), DMA(sems), DMA(sems)],
+        scratch_shapes=[pltpu.VMEM(w.shape, BF), DMA((3,)), pltpu.VMEM((L, 3 * D), BF), DMA((3,)), DMA((M + 1,)), DMA((M,)), DMA((2, M + 1)), DMA((2, M)), DMA(sems), DMA(sems)],
         compiler_params=params_of(1, grid=1),
     )(lengths, x, w, proj, w_in, w_out)
 
@@ -683,13 +695,24 @@
     return x * phi, phi + x * (jnp.exp2((x * x) * (-0.5 * LOG2E)) * 0.3989422804014327)
 
 
-def mlp_kernel(len_ref, x_ref, mixed_ref, cot_ref, params_ref, wproj_ref, win_ref, wout_ref, land_ref,
-               y_ref, mgrad_ref, dmixed_ref, sums_ref, pproj_ref, pin_ref, pout_ref, din_ref, dout_ref, half_ref,
-               w_s, mid_s, hid_s, sg_s, sec_s, br_s, act_s, eg_s, got_s, near_s, diag_s,
+def mlp_kernel(len_ref, x_hbm, mixed_hbm, cot_hbm, params_ref, wproj_hbm, win_ref, wout_ref, land_ref,
+               y_hbm, mgrad_hbm, dmixed_hbm, sums_ref, pproj_ref, pin_ref, pout_ref, din_ref, dout_ref, half_ref,
+               x_ref, mixed_ref, cot_ref, wproj_ref, in_sems, out_sems, w_s, mid_s, hid_s, sg_s, sec_s, br_s, act_s, eg_s, got_s, near_s, diag_s,
                load_sems, save_sems, gsends, grecvs, ssends, srecvs, *, tr):
     at = Place()
     G, M = at.G, at.M
     L, D = x_ref.shape
+    n_rows = L // tr
+    enter_loads = [
+        [pltpu.make_async_copy(src.at[pl.ds(i * tr, tr)], dst.at[pl.ds(i * tr, tr)], in_sems.at[i, j])
+         for j, (src, dst) in enumerate(((mixed_hbm, mixed_ref), (x_hbm, x_ref), (cot_hbm, cot_ref)))]
+        for i in range(n_rows)
+    ]
+    proj_load = pltpu.make_async_copy(wproj_hbm, wproj_ref, in_sems.at[0, 3])
+    proj_load.start()
+    for group in enter_loads:
+        for cp in group:
+            cp.start()
     R, Fb = land_ref.shape[2:]
     half = M // 2
     gain, bias = params_ref[1:2, :], params_ref[3:4, :]
@@ -713,6 +736,10 @@
         return pl.ds(i * tr, tr)
 
     def enter(i):
+        if i == 0:
+            proj_load.wait()
+        for cp in enter_loads[i]:
+            cp.wait()
         sl = rows(i)
         mid = x_ref[sl, :].astype(F32) + dot(mixed_ref[sl, :], wproj_ref[...], NN)
         mid_s[sl, :] = mid
@@ -722,7 +749,6 @@
         br_s[sl, :] = jnp.where(at_row < len_ref[0], cot_ref[sl, :].astype(F32), 0.0).astype(BF)
         sg_s[sl, :] = jnp.zeros((tr, D), F32)
 
-    n_rows = L // tr
     enter(0)
     at.meet()
     for group in gathers:
@@ -795,18 +821,25 @@
     n_back = L // 256 if L % 256 == 0 else 1
     tb = L // n_back
 
+    def saves(i):
+        sl = pl.ds(pl.multiple_of(i * tb, tb), tb)
+        return [pltpu.make_async_copy(src.at[sl], dst.at[sl], out_sems.at[i, j])
+                for j, (src, dst) in enumerate(((x_ref, y_hbm), (mid_s, mgrad_hbm), (cot_ref, dmixed_hbm)))]
+
     def back(i, carry):
         sl = pl.ds(pl.multiple_of(i * tb, tb), tb)
-        y_ref[sl, :] = hid_s[sl, :].astype(BF)
+        x_ref[sl, :] = hid_s[sl, :].astype(BF)
         xhat, r = norm_stats(mid_s[sl, :])
         e = sg_s[sl, :]
         sums_ref[1:2, :] += jnp.sum(e * xhat, axis=0, keepdims=True)
         sums_ref[3:4, :] += jnp.sum(e, axis=0, keepdims=True)
         grad = br_s[sl, :].astype(F32) + norm_pull(e, xhat, r, gain)
-        mgrad_ref[sl, :] = grad
+        mid_s[sl, :] = grad
         low = grad.astype(BF)
         sec_s[sl, :] = low
-        dmixed_ref[sl, :] = dot(low, wproj_ref[...], NT).astype(BF)
+        cot_ref[sl, :] = dot(low, wproj_ref[...], NT).astype(BF)
+        for cp in saves(i):
+            cp.start()
         return carry
 
     lax.fori_loop(0, n_back, back, 0)
@@ -825,6 +858,13 @@
         for a, ref in enumerate((pin_ref, pout_ref)):
             pltpu.make_async_copy(w_s.at[k, a], ref.at[k - 2], save_sems.at[k - 2, a]).wait()
     save_half.wait()
+
+    def saved(i, carry):
+        for cp in saves(i):
+            cp.wait()
+        return carry
+
+    lax.fori_loop(0, n_back, saved, 0)
     for k, group in enumerate(sums):
         for u in group:
             u.finish(True, k == 0)
@@ -839,8 +879,8 @@
     pieces = jax.ShapeDtypeStruct((M - 2, 2 * G) + block, BF)
     return pl.pallas_call(
         functools.partial(mlp_kernel, tr=tr),
-        in_specs=[SMEM, VMEM, VMEM, VMEM, VMEM, VMEM, ANY, ANY, ANY],
-        out_specs=[VMEM] * 5 + [ANY, ANY, VMEM, VMEM, ANY],
+        in_specs=[SMEM, ANY, ANY, ANY, VMEM, ANY, ANY, ANY, ANY],
+        out_specs=[ANY] * 3 + [VMEM] * 2 + [ANY, ANY, VMEM, VMEM, ANY],
         out_shape=[
             jax.ShapeDtypeStruct((L, D), BF),
             jax.ShapeDtypeStruct((L, D), F32),
@@ -851,6 +891,8 @@
             jax.ShapeDtypeStruct(block, F32), jax.ShapeDtypeStruct(block, F32), jax.ShapeDtypeStruct((2, G) + block, BF),
         ],
         scratch_shapes=[
+            pltpu.VMEM((L, D), BF), pltpu.VMEM((L, D), BF), pltpu.VMEM((L, D), BF), pltpu.VMEM((D, D), BF),
+            DMA((L // tr, 4)), DMA((L // 256 if L % 256 == 0 else 1, 3)),
             pltpu.VMEM((M, 2, 2 * G) + block, BF),
             pltpu.VMEM((L, D), F32), pltpu.VMEM((L, D), F32), pltpu.VMEM((L, D), F32),
             pltpu.VMEM((L, D), BF), pltpu.VMEM((L, D), BF), pltpu.VMEM((L, Fb), BF), pltpu.VMEM((L, Fb), BF),
@@ -859,10 +901,10 @@
     )(lengths, x, mixed, cot, params, wproj, win, wout, land)
 
 
-def attend_back_kernel(len_ref, q_ref, k_ref, v_ref, do_ref, wide_ref, lse_ref, normed_ref, pin_ref, pout_ref, pproj_ref, hin_ref, hout_ref, half_ref,
+def attend_back_kernel(len_ref, q_ref, k_ref, v_ref, do_ref, wide_ref, lse_ref, normed_hbm, pin_ref, pout_ref, pproj_ref, hin_ref, hout_ref, half_ref,
                        dqkv_ref, din_ref, dout_ref, dproj_ref, sum_ref, rest_ref,
                        own_m, got_m, near_m, diag_m, send_m, far_in, far_out, own_p, got_p, near_p, diag_p, send_p, far_p,
-                       parts_s, got_q, near_q, diag_q, send_q, far_q, sends, recvs, far_recvs, far_recvs_q, save_sem, *, tq):
+                       parts_s, got_q, near_q, diag_q, send_q, far_q, sends, recvs, far_recvs, far_recvs_q, save_sem, normed_ref, *, tq):
     p, steps = pl.program_id(0), ATTEND_STEPS
     at = Place()
     G, M = at.G, at.M
@@ -908,6 +950,10 @@
         slot = slot + 1 if slot % parts == 0 else slot
         plan.setdefault(min(slot, steps * parts - 1), []).extend(getattr(u, name) for u in group)
 
+    load = pltpu.make_async_copy(normed_hbm, normed_ref, save_sem.at[1])
+    pl.when(p == 0)(load.start)
+    pl.when(p == 1)(load.wait)
+
     def begin():
         din_ref[...], dout_ref[...] = hin_ref[...], hout_ref[...]
 
@@ -919,20 +965,22 @@
         put(1, "start", group)
     for n, group in enumerate(others):
         put(BACK["pair0"] if n == 0 else BACK["pair1"], "pair", group)
-        put(BACK["join0"] if n == 0 else BACK["join1"], "join", group)
+        if n != 1:
+            put(BACK["join0"], "join", group)
     put(BACK["pair_p"], "pair", every(proj))
     put(BACK["join_1"], "join", main[1])
     for group in others[1:]:
         put(BACK["cross1"], "cross", group)
     put(BACK["pair_h0"], "pair", every(heads[0]))
     put(BACK["cross_p"], "cross", every(proj))
+    put(BACK["pair_h1"], "pair", every(heads[1]))
     put(BACK["cross_h0"], "cross", every(heads[0]))
-    put(BACK["pair_h1"], "pair", every(heads[1]))
     put(BACK["join_p"], "join", early(proj))
     put(BACK["cross_h1"], "cross", every(heads[1]))
     put(BACK["late_p"], "join", late(proj))
     put(BACK["join_h0"], "join", early(heads[0]))
     put(BACK["late_h0"], "join", late(heads[0]))
+    put(BACK["join_h1"], "join", early(heads[1]))
     grad_to = lambda t: dqkv_ref.at[0, :, pl.ds(pl.multiple_of(t * 256 + lax.rem(p, 2) * 128, 128), 128)]
     attend_back_step(p, len_ref, q_ref, k_ref, v_ref, do_ref, wide_ref, lse_ref, grad_to(0), grad_to(1), grad_to(2), tq, at_slots(p, parts, plan))
 
@@ -943,7 +991,7 @@
 
     @pl.when(p == steps - 1)
     def _():
-        for u in early(heads[1]):
+        for u in late(heads[1]):
             u.join()
 
     @pl.when(lax.rem(p, 2) == 1)
@@ -964,11 +1012,14 @@
             for u in every(group):
                 u.start()
 
+    @pl.when(p == 3)
+    def _():
+        for u in others[1] if len(others) > 1 else []:
+            u.join()
+
     @pl.when(p == steps - 1)
     def _():
         save.start()
-        for u in late(heads[1]):
-            u.join()
         for u in units:
             u.close()
         for u in units:
@@ -990,7 +1041,7 @@
     return pl.pallas_call(
         functools.partial(attend_back_kernel, tq=tq),
         grid=(pairs,),
-        in_specs=[SMEM, column(0), column(pairs), column(2 * pairs), column(0), column(0), whole((L, 128)), whole((L, D)), ANY, ANY, ANY,
+        in_specs=[SMEM, column(0), column(pairs), column(2 * pairs), column(0), column(0), whole((L, 128)), ANY, ANY, ANY, ANY,
                   whole(mshape), whole(mshape), whole(halfway.shape)],
         out_specs=[pl.BlockSpec((1, L, 768), lambda p: (p // 2, 0, 0)), out(mshape), out(mshape), out(pshape), out((groups - 1,) + pshape), ANY],
         out_shape=[jax.ShapeDtypeStruct((groups, L, 768), BF)]
@@ -998,12 +1049,13 @@
         + [jax.ShapeDtypeStruct(pshape, F32), jax.ShapeDtypeStruct((groups - 1,) + pshape, F32), jax.ShapeDtypeStruct((M, 2, G) + pshape, BF)],
         scratch_shapes=sum_buffers(rest - 2, G, mshape)[:2] + sum_buffers(rest, G, mshape, far=M)[2:] + [pltpu.VMEM((M,) + mshape, BF)] + sum_buffers(M, G, pshape, far=M)
         + [pltpu.VMEM((groups, M, 2, G) + pshape, BF)] + sum_buffers((groups - 1) * M, G, pshape, own=False, far=(groups - 1) * M)
-        + [DMA(sems), DMA(sems), DMA((3, M)), DMA((groups - 1, M)), DMA((1,))],
+        + [DMA(sems), DMA(sems), DMA((3, M)), DMA((groups - 1, M)), DMA((2,)), pltpu.VMEM((L, D), BF)],
         compiler_params=params_of(2, grid=1),
     )(lengths, packed, packed, packed, do, wide, lse, normed, p_in, p_out, p_proj, h_in, h_out, halfway)
 
 
-def exit_kernel(x_ref, dqkv_ref, w_ref, mid_ref, second_ref, params_ref, parts_ref, sums_ref, grad_ref, qkv_ref, norms_ref,
+def exit_kernel(x_hbm, dqkv_hbm, w_hbm, mid_hbm, second_ref, params_ref, parts_hbm, sums_ref, grad_hbm, qkv_ref, norms_ref,
+                x_ref, dqkv_ref, w_ref, mid_ref, parts_ref, load_sems, save_sems,
                 got_s, near_s, diag_s, send_s, far_s, sum_s, norm_s, e_s, small_parts, small_got,
                 sends, recvs, far_recvs, small_sends, small_recvs, *, rows):
     at = Place(everyone=True)
@@ -1011,47 +1063,62 @@
     L, D = x_ref.shape
     R = qkv_ref.shape[0]
     groups = dqkv_ref.shape[0]
+    loads = [
+        [pltpu.make_async_copy(dqkv_hbm.at[g], dqkv_ref.at[g], load_sems.at[g, 0]),
+         pltpu.make_async_copy(w_hbm.at[:, :, pl.ds(g * 256, 256)], w_ref.at[g], load_sems.at[g, 1])]
+        for g in range(groups)
+    ]
+    later = [pltpu.make_async_copy(parts_hbm, parts_ref, load_sems.at[0, 2]), pltpu.make_async_copy(x_hbm, x_ref, load_sems.at[1, 2]),
+             pltpu.make_async_copy(mid_hbm, mid_ref, load_sems.at[2, 2])]
+    for cp in loads[0] + later[:1] + [cp for group in loads[1:] for cp in group] + later[1:]:
+        cp.start()
     small = SmallScatter(at, small_parts, small_got, small_sends, small_recvs)
     units = [
         SumUnit(at, lambda c, n=n: parts_ref.at[at.near[n], c], None, *[b.at[n] for b in (got_s, near_s, diag_s, send_s)], far_s, sum_s, n, n % 2,
                 sends.at[n], recvs.at[n], far_recvs)
         for n in reversed(range(M))
     ]
-    link(units)
-
-    def run(name, ns=tuple(range(8))):
+
+    def run(name):
         for u in units:
-            if u.n in ns or u.n > 7:
-                getattr(u, name)()
+            getattr(u, name)()
 
     gain = params_ref[0:1, :]
-    plan = {0: "start", 1: "pair", 2: "cross"}
-
-    def matmul(g, carry):
-        lane = pl.multiple_of(g * 256, 256)
-
-        def piece(i, carry):
-            sl = pl.ds(pl.multiple_of(i * (L // 2), L // 2), L // 2)
-            e = sum(dot(dqkv_ref[g, sl, t * 256 : t * 256 + 256], w_ref[t, :, pl.ds(lane, 256)], NT) for t in range(3))
-            e_s[sl, :] = e_s[sl, :] + e
-            return carry
-
-        lax.fori_loop(0, 2, piece, 0)
+    plan = {0: "start", 2: "pair", 5: "cross"}
+
+    def matmul(step, carry):
+        g, i = step // 2, lax.rem(step, 2)
+        for j, group in enumerate(loads):
+
+            @pl.when(step == 2 * j)
+            def _(group=group):
+                for cp in group:
+                    cp.wait()
+
+        sl = pl.ds(pl.multiple_of(i * (L // 2), L // 2), L // 2)
+        e = sum(dot(dqkv_ref[g, sl, t * 256 : t * 256 + 256], w_ref[g, t], NT) for t in range(3))
+        e_s[sl, :] = e_s[sl, :] + e
         for j, name in plan.items():
 
-            @pl.when(g == j)
+            @pl.when(step == j)
             def _(j=j, name=name):
                 if j == 0:
+                    later[0].wait()
                     at.meet()
                 run(name)
 
         return carry
+
+    def saves(i):
+        sl = pl.ds(pl.multiple_of(i * rows, rows), rows)
+        return pltpu.make_async_copy(mid_ref.at[sl], grad_hbm.at[sl], save_sems.at[i])
 
     def norm(i, carry):
         sl = pl.ds(pl.multiple_of(i * rows, rows), rows)
         e = e_s[sl, :]
         xhat, r = norm_stats(x_ref[sl, :].astype(F32))
-        grad_ref[sl, :] = mid_ref[sl, :] + norm_pull(e, xhat, r, gain)
+        mid_ref[sl, :] = mid_ref[sl, :] + norm_pull(e, xhat, r, gain)
+        saves(i).start()
         norm_s[0:1, :] += jnp.sum(e * xhat, axis=0, keepdims=True)
         norm_s[2:3, :] += jnp.sum(e, axis=0, keepdims=True)
         return carry
@@ -1059,20 +1126,27 @@
     at.greet()
     norm_s[...] = second_ref[...]
     e_s[...] = jnp.zeros_like(e_s)
-    lax.fori_loop(0, groups, matmul, 0)
+    lax.fori_loop(0, 2 * groups, matmul, 0)
+    for cp in later[1:]:
+        cp.wait()
     lax.fori_loop(0, L // rows, norm, 0)
     small.start(norm_s[...], R)
-    run("join", (0, 1, 3, 4, 5, 6, 7))
+    run("join")
     for g in range(groups - 1):
         for t in range(3):
             qkv_ref[:, pl.ds(t * D + g * 256, 256)] = sums_ref[g, :, pl.ds(t * 256, 256)]
-    run("join", (2,))
     norms_ref[...] = small.collect()
     run("close")
     for t in range(3):
         qkv_ref[:, pl.ds(t * D + (groups - 1) * 256, 256)] = sum_s[:, pl.ds(t * 256, 256)]
     run("finish")
     small.finish()
+
+    def saved(i, carry):
+        saves(i).wait()
+        return carry
+
+    lax.fori_loop(0, L // rows, saved, 0)
 
 
 def leave(x, dqkv, w, middle_grad, second_sums, params, parts, sums):
@@ -1083,14 +1157,17 @@
     sems = (M, SumUnit.count(G))
     return pl.pallas_call(
         functools.partial(exit_kernel, rows=min(256, L)),
-        in_specs=[VMEM] * 8,
-        out_specs=[VMEM] * 3,
+        in_specs=[ANY] * 4 + [VMEM, VMEM, ANY, VMEM],
+        out_specs=[ANY, VMEM, VMEM],
         out_shape=[
             jax.ShapeDtypeStruct((L, D), F32),
             jax.ShapeDtypeStruct((R, 3 * D), F32),
             jax.ShapeDtypeStruct((8, 128), F32),
         ],
-        scratch_shapes=sum_buffers(M, G, (R, D), own=False, far=M)
+        scratch_shapes=[
+            pltpu.VMEM((L, D), BF), pltpu.VMEM(dqkv.shape, BF), pltpu.VMEM((dqkv.shape[0], 3, D, 256), BF), pltpu.VMEM((L, D), F32),
+            pltpu.VMEM(parts.shape, BF), DMA((3, 3)), DMA((L // min(256, L),)),
+        ] + sum_buffers(M, G, (R, D), own=False, far=M)
         + [pltpu.VMEM((R, D), F32), pltpu.VMEM((8, D), F32), pltpu.VMEM((L, D), F32), pltpu.VMEM((n, 8, 128), F32), pltpu.VMEM((n, 8, 128), F32),
            DMA(sems), DMA(sems), DMA((M,)), DMA((n,)), DMA((n,))],
         compiler_params=params_of(3),

time: 236 us -> 229 us (0.970)
  Pallas kernels: 226 us -> 219 us
    pallas_call x1, Pallas kernels: 27.2 us -> 21.3 us  [leave(): pl.pallas_call(functools.partial(exit_kernel, rows=min(256, L)), in_specs...]
    pallas_call x1, Pallas kernels: 55.2 us -> 52.4 us  [mlp(): pl.pallas_call(functools.partial(mlp_kernel, tr=tr), in_specs=[SMEM, ANY,...]
    pallas_call x1, Pallas kernels: 64.8 us -> 67.6 us  [attend_back(): pl.pallas_call(functools.partial(attend_back_kernel, tq=tq), grid=(pairs,...]
where the time goes in v3:
time: 229 us
  Pallas kernels  219 us (96%)
  local copies, waits for them, and re-layouts  8.2 us (4%)
    pallas_call x1, Pallas kernels, attend_back(): pl.pallas_call(functools.partial(attend_back_kernel, tq=tq), grid=(pairs,...  67.6 us
    pallas_call x1, Pallas kernels, mlp(): pl.pallas_call(functools.partial(mlp_kernel, tr=tr), in_specs=[SMEM, ANY,...  52.4 us
    pallas_call x1, Pallas kernels, attend(): pl.pallas_call(functools.partial(attend_kernel, tq=tq), grid=(D // 128,),...  42.6 us
    pallas_call x1, Pallas kernels, entry(): pl.pallas_call(functools.partial(entry_kernel, rows=min(256, L)), in_spec...  35.1 us
    pallas_call x1, Pallas kernels, leave(): pl.pallas_call(functools.partial(exit_kernel, rows=min(256, L)), in_specs...  21.3 us
    unnamed x18, local copies, waits for them, and re-layouts  6.89 us

profile of v3, /device:TPU:0, one launch (start us, length us, event | category | flops | bytes accessed | tf_op | source)
XLA Modules:
  0.0 228.6 jit_solution(18441935803286972266)
XLA Ops:
  1.3 35.1 %shard_map.152 = (bf16[3,4,2,4,24,768]{5,4,3,2,1,0:T(8,128)(2,1)}, bf16[1024,768]{1,0:T(8,128)(2,1)}, f32[8,768]{1,0:T(8,128)}) custom-call(bf16[1024,768]{1,0:T(8,128)(2,1)} %x_hbm.3, bf16[24,2304]{1,0:T(8,128)(2,1)} %bitcast.32, bf16[2,24]{1,0:T(2,128)(2,1)} %bitcast.35, bf16[2,24]{1,0:T(2,128)(2,1)} %bitcast.36), custom_call_target="tpu_custom_call" | custom-call | tf_op jit(solution)/shard_map/pallas_call | solution.py:434
  36.4 42.6 %shard_map.153 = (bf16[1024,768]{1,0:T(8,128)(2,1)}, f32[1024,768]{1,0:T(8,128)}, f32[1024,128]{1,0:T(8,128)}, bf16[1024,2304]{1,0:T(8,128)(2,1)}, bf16[4,2,4,24...) custom-call(s32[1]{0:T(128)S(6)} %copy.23.len_ref, ...), custom_call_target="tpu_custom_call" | custom-call | tf_op jit(solution)/shard_map/pallas_call | solution.py:674
  79.1 52.4 %shard_map.154 = (bf16[1024,768]{1,0:T(8,128)(2,1)}, f32[1024,768]{1,0:T(8,128)}, bf16[1024,768]{1,0:T(8,128)(2,1)}, f32[8,768]{1,0:T(8,128)}, bf16[4,2,4,24,768...) custom-call(s32[1]{0:T(128)S(6)} %copy.23.len_ref, ...), custom_call_target="tpu_custom_call" | custom-call | tf_op jit(solution)/shard_map/pallas_call | solution.py:880
  131.5 67.6 %shard_map.155 = (bf16[3,1024,768]{2,1,0:T(8,128)(2,1)}, f32[96,768]{1,0:T(8,128)}, f32[96,768]{1,0:T(8,128)}, f32[24,768]{1,0:T(8,128)}, f32[2,24,768]{2,1,0:T(8,128)}, /*index=5*/bf16[4,2,4,24,768]{4,3,2,1,0:T(8,128)(2,1)}) custom-call(s32[1]{0:T(128)S(6)} %copy.23.len_ref, bf16[1024,2304]{1,0:T(8,128)(2,1)} %get-tuple-element.47.q_ref.k_ref.v_ref, ...), custom_call_target="tpu_custom_call" | custom-call | tf_op jit(solution)/shard_map/pallas_call | solution.py:1041
  199.1 0.0 copy-start.1
  199.1 21.3 %shard_map.156 = (f32[1024,768]{1,0:T(8,128)}, f32[24,2304]{1,0:T(8,128)}, f32[8,128]{1,0:T(8,128)}) custom-call(bf16[1024,768]{1,0:T(8,128)(2,1)} %x_hbm.3, bf16[3,1024,768]{2,1,0:T(8,128)(2,1)} %get-tuple-element.57.dqkv_hbm, bf16[3,768,768]{2,1,0:T(8,128)(2,1)} %bitcast.23, f32[1024,768]{1,0:T(8,128)} %get-tuple-element.58.mid_hbm, ...), custom_call_target="tpu_custom_call" | custom-call | tf_op jit(solution)/shard_map/pallas_call | solution.py:1158
  220.4 1.3 slice_bitcast_fusion
  221.7 0.0 copy-done.1
  221.7 0.0 copy-start
  221.7 1.1 copy.24
  222.9 1.3 copy-done
  224.2 0.0 copy-start.4
  224.2 0.0 copy-start.5
  224.2 0.0 copy-start.3
  224.2 0.0 copy-start.2
  224.2 1.7 copy.25
  225.8 0.0 copy-done.4
  225.8 0.7 copy.26
  226.5 0.0 copy-done.5
  226.5 0.6 copy.27
  227.2 0.0 copy-done.3
  227.2 0.7 copy.28
  227.9 0.0 copy-done.2
  227.9 0.7 copy.29
Async XLA Ops:
  199.1 22.6 %copy-start.1 = (bf16[1024,768]{1,0:T(8,128)(2,1)S(1)}, bf16[1024,768]{1,0:T(8,128)(2,1)}, u32[]{:S(2)}) copy-start(bf16[1024,768]{1,0:T(8,128)(2,1)} %get-tuple-element.78) | copy-start | bytes 4718596
  221.7 2.5 %copy-start = (f32[1024,768]{1,0:T(8,128)S(1)}, f32[1024,768]{1,0:T(8,128)}, u32[]{:S(2)}) copy-start(f32[1024,768]{1,0:T(8,128)} %get-tuple-element.79) | copy-start | bytes 9437188
  224.2 1.7 copy-start.4
  224.2 2.4 %copy-start.5 = (f32[24,768]{1,0:T(8,128)S(1)}, f32[24,768]{1,0:T(8,128)}, u32[]{:S(2)}) copy-start(f32[24,768]{1,0:T(8,128)} %get-tuple-element.64) | copy-start | bytes 221188
  224.2 3.0 %copy-start.3 = (f32[96,768]{1,0:T(8,128)S(1)}, f32[96,768]{1,0:T(8,128)}, u32[]{:S(2)}) copy-start(f32[96,768]{1,0:T(8,128)} %get-tuple-element.65) | copy-start | bytes 884740
  224.2 3.7 %copy-start.2 = (f32[96,768]{1,0:T(8,128)S(1)}, f32[96,768]{1,0:T(8,128)}, u32[]{:S(2)}) copy-start(f32[96,768]{1,0:T(8,128)} %get-tuple-element.66) | copy-start | bytes 884740

commit v4 on v3

--- a/solution.py
+++ b/solution.py
@@ -656,11 +656,10 @@
 
 
 ATTEND_STEPS = 6
-ATTEND_PROJ = [[0, 2, 5], [1, 5, 8], [4, 7, 10], [6, 9, 11]]
-ATTEND_MAIN = [[[0, 4, 8], [0, 4, 8]], [[3, 7, 11], [4, 8, 11]]]
-BACK = {"pair0": 5, "pair1": 6, "pair_p": 7, "join_1": 7, "cross1": 9, "pair_h0": 10, "cross_p": 11, "join0": 13, "cross_h0": 17,
-        "pair_h1": 17, "join_p": 19, "cross_h1": 19, "late_p": 21, "join_h0": 21, "late_h0": 23, "join_h1": 23}
-MLP = {"relay0": (0, 3), "spread1": (0, 3), "relay1": (1, 3), "last0": (1, 2), "last1": (2, 2), "pair0": (1, 2), "cross0": (2, 1), "pair1": (2, 3), "join0": (3, 1)}
+ATTEND_PROJ = [[0, 0, 4], [0, 4, 6], [4, 6, 8], [6, 8, 10]]
+ATTEND_MAIN = [[[0, 4, 8], [0, 4, 8]], [[2, 8, 10], [4, 8, 10]]]
+BACK = {"pair0": 1, "pair1": 1, "pair_p": 1, "cross1": 2, "pair_h0": 3, "cross_p": 3, "join0": 3, "pair_h1": 4, "join_p": 4, "cross_h1": 5, "late_p": 5, "join_h0": 5}
+MLP = {"relay0": (0, 2), "spread1": (0, 2), "relay1": (2, 0), "last0": (1, 2), "last1": (2, 2), "pair0": (1, 2), "cross0": (2, 2), "pair1": (3, 0), "join0": (3, 2)}
 
 
 def attend(lengths, x, w, proj, w_in, w_out, tq):
@@ -946,9 +945,8 @@
     late = lambda group: [group[n] for n in group if n == 2]
     plan = {}
 
-    def put(slot, name, group):
-        slot = slot + 1 if slot % parts == 0 else slot
-        plan.setdefault(min(slot, steps * parts - 1), []).extend(getattr(u, name) for u in group)
+    def put(step, name, group):
+        plan.setdefault(step * parts, []).extend(getattr(u, name) for u in group)
 
     load = pltpu.make_async_copy(normed_hbm, normed_ref, save_sem.at[1])
     pl.when(p == 0)(load.start)
@@ -957,30 +955,25 @@
     def begin():
         din_ref[...], dout_ref[...] = hin_ref[...], hout_ref[...]
 
-    plan[0] = [at.greet, begin]
-    plan[1] = [at.meet]
-    put(1, "launch", main[1])
+    plan[0] = [at.greet, begin, at.meet]
+    put(0, "launch", main[1])
     others = [main[n] for n in reversed(range(2, M))]
     for group in others + [every(proj)]:
-        put(1, "start", group)
+        put(0, "start", group)
     for n, group in enumerate(others):
         put(BACK["pair0"] if n == 0 else BACK["pair1"], "pair", group)
         if n != 1:
             put(BACK["join0"], "join", group)
     put(BACK["pair_p"], "pair", every(proj))
-    put(BACK["join_1"], "join", main[1])
     for group in others[1:]:
         put(BACK["cross1"], "cross", group)
     put(BACK["pair_h0"], "pair", every(heads[0]))
     put(BACK["cross_p"], "cross", every(proj))
+    put(BACK["join_p"], "join", early(proj))
     put(BACK["pair_h1"], "pair", every(heads[1]))
-    put(BACK["cross_h0"], "cross", every(heads[0]))
-    put(BACK["join_p"], "join", early(proj))
     put(BACK["cross_h1"], "cross", every(heads[1]))
     put(BACK["late_p"], "join", late(proj))
     put(BACK["join_h0"], "join", early(heads[0]))
-    put(BACK["late_h0"], "join", late(heads[0]))
-    put(BACK["join_h1"], "join", early(heads[1]))
     grad_to = lambda t: dqkv_ref.at[0, :, pl.ds(pl.multiple_of(t * 256 + lax.rem(p, 2) * 128, 128), 128)]
     attend_back_step(p, len_ref, q_ref, k_ref, v_ref, do_ref, wide_ref, lse_ref, grad_to(0), grad_to(1), grad_to(2), tq, at_slots(p, parts, plan))
 
@@ -988,10 +981,17 @@
     def _():
         for u in others[0]:
             u.cross()
+        for u in main[1]:
+            u.join()
+
+    @pl.when(p == 3)
+    def _():
+        for u in every(heads[0]):
+            u.cross()
 
     @pl.when(p == steps - 1)
     def _():
-        for u in late(heads[1]):
+        for u in late(heads[0]) + early(heads[1]):
             u.join()
 
     @pl.when(lax.rem(p, 2) == 1)
@@ -1020,6 +1020,8 @@
     @pl.when(p == steps - 1)
     def _():
         save.start()
+        for u in late(heads[1]):
+            u.join()
         for u in units:
             u.close()
         for u in units:

time: 229 us -> 222 us (0.969)
  Pallas kernels: 219 us -> 213 us
    pallas_call x1, Pallas kernels: 67.6 us -> 62.9 us  [attend_back(): pl.pallas_call(functools.partial(attend_back_kernel, tq=tq), grid=(pairs,...]
    pallas_call x1, Pallas kernels: 52.4 us -> 49.6 us  [mlp(): pl.pallas_call(functools.partial(mlp_kernel, tr=tr), in_specs=[SMEM, ANY,...]
where the time goes in v4:
time: 222 us
  Pallas kernels  213 us (96%)
  local copies, waits for them, and re-layouts  8.2 us (4%)
    pallas_call x1, Pallas kernels, attend_back(): pl.pallas_call(functools.partial(attend_back_kernel, tq=tq), grid=(pairs,...  62.9 us
    pallas_call x1, Pallas kernels, mlp(): pl.pallas_call(functools.partial(mlp_kernel, tr=tr), in_specs=[SMEM, ANY,...  49.6 us
    pallas_call x1, Pallas kernels, attend(): pl.pallas_call(functools.partial(attend_kernel, tq=tq), grid=(D // 128,),...  43.1 us
    pallas_call x1, Pallas kernels, entry(): pl.pallas_call(functools.partial(entry_kernel, rows=min(256, L)), in_spec...  35.1 us
    pallas_call x1, Pallas kernels, leave(): pl.pallas_call(functools.partial(exit_kernel, rows=min(256, L)), in_specs...  21.7 us
    unnamed x18, local copies, waits for them, and re-layouts  6.89 us

profile of v4, /device:TPU:0, one launch (start us, length us, event | category | flops | bytes accessed | tf_op | source)
XLA Modules:
  0.0 222.1 jit_solution(1176325383115073285)
XLA Ops:
  1.3 35.1 %shard_map.152 = (bf16[3,4,2,4,24,768]{5,4,3,2,1,0:T(8,128)(2,1)}, bf16[1024,768]{1,0:T(8,128)(2,1)}, f32[8,768]{1,0:T(8,128)}) custom-call(bf16[1024,768]{1,0:T(8,128)(2,1)} %x_hbm.3, bf16[24,2304]{1,0:T(8,128)(2,1)} %bitcast.32, bf16[2,24]{1,0:T(2,128)(2,1)} %bitcast.35, bf16[2,24]{1,0:T(2,128)(2,1)} %bitcast.36), custom_call_target="tpu_custom_call" | custom-call | tf_op jit(solution)/shard_map/pallas_call | solution.py:434
  36.4 43.1 %shard_map.153 = (bf16[1024,768]{1,0:T(8,128)(2,1)}, f32[1024,768]{1,0:T(8,128)}, f32[1024,128]{1,0:T(8,128)}, bf16[1024,2304]{1,0:T(8,128)(2,1)}, bf16[4,2,4,24...) custom-call(s32[1]{0:T(128)S(6)} %copy.23.len_ref, ...), custom_call_target="tpu_custom_call" | custom-call | tf_op jit(solution)/shard_map/pallas_call | solution.py:673
  79.6 49.6 %shard_map.154 = (bf16[1024,768]{1,0:T(8,128)(2,1)}, f32[1024,768]{1,0:T(8,128)}, bf16[1024,768]{1,0:T(8,128)(2,1)}, f32[8,768]{1,0:T(8,128)}, bf16[4,2,4,24,768...) custom-call(s32[1]{0:T(128)S(6)} %copy.23.len_ref, ...), custom_call_target="tpu_custom_call" | custom-call | tf_op jit(solution)/shard_map/pallas_call | solution.py:879
  129.2 62.9 %shard_map.155 = (bf16[3,1024,768]{2,1,0:T(8,128)(2,1)}, f32[96,768]{1,0:T(8,128)}, f32[96,768]{1,0:T(8,128)}, f32[24,768]{1,0:T(8,128)}, f32[2,24,768]{2,1,0:T(8,128)}, /*index=5*/bf16[4,2,4,24,768]{4,3,2,1,0:T(8,128)(2,1)}) custom-call(s32[1]{0:T(128)S(6)} %copy.23.len_ref, bf16[1024,2304]{1,0:T(8,128)(2,1)} %get-tuple-element.47.q_ref.k_ref.v_ref, ...), custom_call_target="tpu_custom_call" | custom-call | tf_op jit(solution)/shard_map/pallas_call | solution.py:1043
  192.2 0.0 copy-start.1
  192.2 21.7 %shard_map.156 = (f32[1024,768]{1,0:T(8,128)}, f32[24,2304]{1,0:T(8,128)}, f32[8,128]{1,0:T(8,128)}) custom-call(bf16[1024,768]{1,0:T(8,128)(2,1)} %x_hbm.3, bf16[3,1024,768]{2,1,0:T(8,128)(2,1)} %get-tuple-element.57.dqkv_hbm, bf16[3,768,768]{2,1,0:T(8,128)(2,1)} %bitcast.23, f32[1024,768]{1,0:T(8,128)} %get-tuple-element.58.mid_hbm, ...), custom_call_target="tpu_custom_call" | custom-call | tf_op jit(solution)/shard_map/pallas_call | solution.py:1160
  213.9 1.3 slice_bitcast_fusion
  215.2 0.0 copy-done.1
  215.2 0.0 copy-start
  215.2 1.1 copy.24
  216.4 1.3 copy-done
  217.7 0.0 copy-start.4
  217.7 0.0 copy-start.5
  217.7 0.0 copy-start.3
  217.7 0.0 copy-start.2
  217.7 1.7 copy.25
  219.3 0.0 copy-done.4
  219.3 0.7 copy.26
  220.0 0.0 copy-done.5
  220.0 0.6 copy.27
  220.7 0.0 copy-done.3
  220.7 0.7 copy.28
  221.4 0.0 copy-done.2
  221.4 0.7 copy.29
Async XLA Ops:
  192.2 23.0 %copy-start.1 = (bf16[1024,768]{1,0:T(8,128)(2,1)S(1)}, bf16[1024,768]{1,0:T(8,128)(2,1)}, u32[]{:S(2)}) copy-start(bf16[1024,768]{1,0:T(8,128)(2,1)} %get-tuple-element.78) | copy-start | bytes 4718596
  215.2 2.5 %copy-start = (f32[1024,768]{1,0:T(8,128)S(1)}, f32[1024,768]{1,0:T(8,128)}, u32[]{:S(2)}) copy-start(f32[1024,768]{1,0:T(8,128)} %get-tuple-element.79) | copy-start | bytes 9437188
  217.7 1.7 copy-start.4
  217.7 2.4 %copy-start.5 = (f32[24,768]{1,0:T(8,128)S(1)}, f32[24,768]{1,0:T(8,128)}, u32[]{:S(2)}) copy-start(f32[24,768]{1,0:T(8,128)} %get-tuple-element.64) | copy-start | bytes 221188
  217.7 3.0 %copy-start.3 = (f32[96,768]{1,0:T(8,128)S(1)}, f32[96,768]{1,0:T(8,128)}, u32[]{:S(2)}) copy-start(f32[96,768]{1,0:T(8,128)} %get-tuple-element.65) | copy-start | bytes 884740
  217.7 3.7 %copy-start.2 = (f32[96,768]{1,0:T(8,128)S(1)}, f32[96,768]{1,0:T(8,128)}, u32[]{:S(2)}) copy-start(f32[96,768]{1,0:T(8,128)} %get-tuple-element.66) | copy-start | bytes 884740

commit v5 on v4

--- a/solution.py
+++ b/solution.py
@@ -103,8 +103,8 @@
     def arrive(self, n):
         self._copy(n, self.at.near[n]).wait_recv()
 
-    def finish(self):
-        for n in range(1, self.at.M):
+    def finish(self, ns=None):
+        for n in range(1, self.at.M) if ns is None else ns:
             self._copy(n, self.at.z).wait_send()
 
 
@@ -570,6 +570,7 @@
     parts = x_ref.shape[0] // tq
     land = [lambda s, a=a: land_ref.at[s, a] for a in range(2)]
     own = (in_ref, out_ref)
+    direct = [n for n in range(1, M) if M != 4 or n < 3]
     pland = lambda s: wproj_ref.at[at.g, at.c, s]
     pchain = Along(at, proj_ref, pland, pchain_sends, pchain_recvs)
     chains = [Along(at, own[a], land[a], chain_sends.at[a], chain_recvs.at[a]) for a in range(2)]
@@ -600,7 +601,7 @@
         third(0)
         at.meet()
         pchain.start(*range(1, M))
-        for n in range(1, M):
+        for n in direct:
             for chain in chains:
                 chain.start(n)
         proj[0].spread()
@@ -644,12 +645,14 @@
 
     @pl.when(p == steps - 1)
     def _():
-        for n in range(half, M):
+        for n in direct[half - 1 :]:
             for chain in chains:
                 chain.arrive(n)
-        for group in main + [proj, chains, [pchain]]:
+        for group in main + [proj, [pchain]]:
             for u in group:
                 u.finish()
+        for chain in chains:
+            chain.finish(direct)
         save.wait()
         for cp in own_land:
             cp.wait()
@@ -696,7 +699,7 @@
 
 def mlp_kernel(len_ref, x_hbm, mixed_hbm, cot_hbm, params_ref, wproj_hbm, win_ref, wout_ref, land_ref,
                y_hbm, mgrad_hbm, dmixed_hbm, sums_ref, pproj_ref, pin_ref, pout_ref, din_ref, dout_ref, half_ref,
-               x_ref, mixed_ref, cot_ref, wproj_ref, in_sems, out_sems, w_s, mid_s, hid_s, sg_s, sec_s, br_s, act_s, eg_s, got_s, near_s, diag_s,
+               x_ref, mixed_ref, cot_ref, wproj_ref, in_sems, out_sems, w_s, mid_s, hid_s, sg_s, sec_s, br_s, act_s, eg_s, got_s, near_s, diag_s, last_s, hand_sems,
                load_sems, save_sems, gsends, grecvs, ssends, srecvs, *, tr):
     at = Place()
     G, M = at.G, at.M
@@ -720,7 +723,7 @@
         cp.start()
     at.greet()
     gathers = [
-        [GatherUnit(at, land_ref.at[at.near[k], a], lambda g, c, k=k, a=a: w_s.at[k, a, g * 2 + c], a, gsends.at[k - half, a], grecvs.at[k - half, a])
+        [GatherUnit(at, last_s.at[a] if M == 4 and k == 3 else land_ref.at[at.near[k], a], lambda g, c, k=k, a=a: w_s.at[k, a, g * 2 + c], a, gsends.at[k - half, a], grecvs.at[k - half, a])
          for a in range(2)]
         for k in range(half, M)
     ]
@@ -730,6 +733,8 @@
          for a, total in enumerate((din_ref, dout_ref))]
         for k in range(2)
     ]
+
+    hand = [remote(land_ref.at[at.near[2], a], last_s.at[a], hand_sems.at[0, a], hand_sems.at[1, a], at.along(at.near[1])) for a in range(2)] if M == 4 else []
 
     def rows(i):
         return pl.ds(i * tr, tr)
@@ -750,10 +755,12 @@
 
     enter(0)
     at.meet()
-    for group in gathers:
-        group[0].spread()
-        if group is gathers[0]:
-            group[1].spread()
+    for cp in hand:
+        cp.start()
+    for n, group in enumerate(gathers):
+        for u in group:
+            if n == 0 or not hand:
+                u.spread()
     for i in range(1, n_rows):
         enter(i)
     for cp in loads:
@@ -767,8 +774,9 @@
     for n, group in enumerate(gathers):
         after = lambda name: (MLP[name + "0"] if n == 0 else (MLP[name + "1"][0] + n - 1, MLP[name + "1"][1]))
         put(*after("relay"), "relay", group)
-        if n:
-            put(*MLP["spread1"], "spread", group[1:])
+        if n and hand:
+            plan.setdefault(MLP["spread1"], []).extend([cp.wait_recv for cp in hand])
+            put(*MLP["spread1"], "spread", group)
         put(*after("last"), "last", group)
         put(half + n, 0, "finish", group)
     put(1, 0, "start", sums[0])
@@ -867,6 +875,8 @@
     for k, group in enumerate(sums):
         for u in group:
             u.finish(True, k == 0)
+    for cp in hand:
+        cp.wait_send()
 
 
 def mlp(lengths, x, mixed, cot, params, wproj, win, wout, land, R_p, tr):
@@ -895,7 +905,7 @@
             pltpu.VMEM((M, 2, 2 * G) + block, BF),
             pltpu.VMEM((L, D), F32), pltpu.VMEM((L, D), F32), pltpu.VMEM((L, D), F32),
             pltpu.VMEM((L, D), BF), pltpu.VMEM((L, D), BF), pltpu.VMEM((L, Fb), BF), pltpu.VMEM((L, Fb), BF),
-        ] + sum_buffers(4, G, block, own=False)[:3] + [DMA((half, 2)), DMA((M - 2, 2)), DMA(gsems), DMA(gsems), DMA(ssems), DMA(ssems)],
+        ] + sum_buffers(4, G, block, own=False)[:3] + [pltpu.VMEM((2,) + block, BF), DMA((2, 2)), DMA((half, 2)), DMA((M - 2, 2)), DMA(gsems), DMA(gsems), DMA(ssems), DMA(ssems)],
         compiler_params=params_of(4),
     )(lengths, x, mixed, cot, params, wproj, win, wout, land)
 

time: 222 us -> 221 us (level)
  no operation moved by 1% of the time
where the time goes in v5:
time: 221 us
  Pallas kernels  211 us (95%)
  local copies, waits for them, and re-layouts  8.2 us (4%)
    pallas_call x1, Pallas kernels, attend_back(): pl.pallas_call(functools.partial(attend_back_kernel, tq=tq), grid=(pairs,...  63.4 us
    pallas_call x1, Pallas kernels, mlp(): pl.pallas_call(functools.partial(mlp_kernel, tr=tr), in_specs=[SMEM, ANY,...  48.2 us
    pallas_call x1, Pallas kernels, attend(): pl.pallas_call(functools.partial(attend_kernel, tq=tq), grid=(D // 128,),...  43.1 us
    pallas_call x1, Pallas kernels, entry(): pl.pallas_call(functools.partial(entry_kernel, rows=min(256, L)), in_spec...  35.1 us
    pallas_call x1, Pallas kernels, leave(): pl.pallas_call(functools.partial(exit_kernel, rows=min(256, L)), in_specs...  21.3 us
    unnamed x18, local copies, waits for them, and re-layouts  6.89 us

profile of v5, /device:TPU:0, one launch (start us, length us, event | category | flops | bytes accessed | tf_op | source)
XLA Modules:
  0.0 220.7 jit_solution(4197338728070698477)
XLA Ops:
  1.3 35.1 %shard_map.152 = (bf16[3,4,2,4,24,768]{5,4,3,2,1,0:T(8,128)(2,1)}, bf16[1024,768]{1,0:T(8,128)(2,1)}, f32[8,768]{1,0:T(8,128)}) custom-call(bf16[1024,768]{1,0:T(8,128)(2,1)} %x_hbm.3, bf16[24,2304]{1,0:T(8,128)(2,1)} %bitcast.32, bf16[2,24]{1,0:T(2,128)(2,1)} %bitcast.35, bf16[2,24]{1,0:T(2,128)(2,1)} %bitcast.36), custom_call_target="tpu_custom_call" | custom-call | tf_op jit(solution)/shard_map/pallas_call | solution.py:434
  36.4 43.1 %shard_map.153 = (bf16[1024,768]{1,0:T(8,128)(2,1)}, f32[1024,768]{1,0:T(8,128)}, f32[1024,128]{1,0:T(8,128)}, bf16[1024,2304]{1,0:T(8,128)(2,1)}, bf16[4,2,4,24...) custom-call(s32[1]{0:T(128)S(6)} %copy.23.len_ref, ...), custom_call_target="tpu_custom_call" | custom-call | tf_op jit(solution)/shard_map/pallas_call | solution.py:676
  79.6 48.2 %shard_map.154 = (bf16[1024,768]{1,0:T(8,128)(2,1)}, f32[1024,768]{1,0:T(8,128)}, bf16[1024,768]{1,0:T(8,128)(2,1)}, f32[8,768]{1,0:T(8,128)}, bf16[4,2,4,24,768...) custom-call(s32[1]{0:T(128)S(6)} %copy.23.len_ref, ...), custom_call_target="tpu_custom_call" | custom-call | tf_op jit(solution)/shard_map/pallas_call | solution.py:889
  127.8 63.4 %shard_map.155 = (bf16[3,1024,768]{2,1,0:T(8,128)(2,1)}, f32[96,768]{1,0:T(8,128)}, f32[96,768]{1,0:T(8,128)}, f32[24,768]{1,0:T(8,128)}, f32[2,24,768]{2,1,0:T(8,128)}, /*index=5*/bf16[4,2,4,24,768]{4,3,2,1,0:T(8,128)(2,1)}) custom-call(s32[1]{0:T(128)S(6)} %copy.23.len_ref, bf16[1024,2304]{1,0:T(8,128)(2,1)} %get-tuple-element.47.q_ref.k_ref.v_ref, ...), custom_call_target="tpu_custom_call" | custom-call | tf_op jit(solution)/shard_map/pallas_call | solution.py:1053
  191.2 0.0 copy-start.1
  191.2 21.3 %shard_map.156 = (f32[1024,768]{1,0:T(8,128)}, f32[24,2304]{1,0:T(8,128)}, f32[8,128]{1,0:T(8,128)}) custom-call(bf16[1024,768]{1,0:T(8,128)(2,1)} %x_hbm.3, bf16[3,1024,768]{2,1,0:T(8,128)(2,1)} %get-tuple-element.57.dqkv_hbm, bf16[3,768,768]{2,1,0:T(8,128)(2,1)} %bitcast.23, f32[1024,768]{1,0:T(8,128)} %get-tuple-element.58.mid_hbm, ...), custom_call_target="tpu_custom_call" | custom-call | tf_op jit(solution)/shard_map/pallas_call | solution.py:1170
  212.5 1.3 slice_bitcast_fusion
  213.8 0.0 copy-done.1
  213.8 0.0 copy-start
  213.8 1.1 copy.24
  214.9 1.3 copy-done
  216.2 0.0 copy-start.4
  216.2 0.0 copy-start.5
  216.2 0.0 copy-start.3
  216.3 0.0 copy-start.2
  216.3 1.7 copy.25
  217.9 0.0 copy-done.4
  217.9 0.7 copy.26
  218.6 0.0 copy-done.5
  218.6 0.6 copy.27
  219.2 0.0 copy-done.3
  219.2 0.7 copy.28
  220.0 0.0 copy-done.2
  220.0 0.7 copy.29
Async XLA Ops:
  191.2 22.6 %copy-start.1 = (bf16[1024,768]{1,0:T(8,128)(2,1)S(1)}, bf16[1024,768]{1,0:T(8,128)(2,1)}, u32[]{:S(2)}) copy-start(bf16[1024,768]{1,0:T(8,128)(2,1)} %get-tuple-element.78) | copy-start | bytes 4718596
  213.8 2.5 %copy-start = (f32[1024,768]{1,0:T(8,128)S(1)}, f32[1024,768]{1,0:T(8,128)}, u32[]{:S(2)}) copy-start(f32[1024,768]{1,0:T(8,128)} %get-tuple-element.79) | copy-start | bytes 9437188
  216.2 1.7 copy-start.4
  216.2 2.4 %copy-start.5 = (f32[24,768]{1,0:T(8,128)S(1)}, f32[24,768]{1,0:T(8,128)}, u32[]{:S(2)}) copy-start(f32[24,768]{1,0:T(8,128)} %get-tuple-element.64) | copy-start | bytes 221188
  216.2 3.0 %copy-start.3 = (f32[96,768]{1,0:T(8,128)S(1)}, f32[96,768]{1,0:T(8,128)}, u32[]{:S(2)}) copy-start(f32[96,768]{1,0:T(8,128)} %get-tuple-element.65) | copy-start | bytes 884740
  216.3 3.7 %copy-start.2 = (f32[96,768]{1,0:T(8,128)S(1)}, f32[96,768]{1,0:T(8,128)}, u32[]{:S(2)}) copy-start(f32[96,768]{1,0:T(8,128)} %get-tuple-element.66) | copy-start | bytes 884740

commit v6 on v5

--- a/solution.py
+++ b/solution.py
@@ -373,10 +373,12 @@
     return r * (y - jnp.mean(y, axis=-1, keepdims=True) - xhat * jnp.mean(y * xhat, axis=-1, keepdims=True))
 
 
-def entry_kernel(x_ref, block_ref, gain_ref, bias_ref, w_ref, normed_ref, params_ref, shard_ref, own_ref, got, chain_sends, chain_recvs, sends, recvs,
+def entry_kernel(x_hbm, block_ref, gain_ref, bias_ref, w_ref, normed_ref, params_ref, x_ref, load_sem, shard_ref, own_ref, got, chain_sends, chain_recvs, sends, recvs,
                  small_sends, small_recvs, *, rows):
     at = Place(everyone=True)
     at.greet()
+    load = pltpu.make_async_copy(x_hbm, x_ref, load_sem.at[0])
+    load.start()
     land = lambda s: w_ref.at[:, at.g, at.c, s]
     chain = Along(at, shard_ref, land, chain_sends, chain_recvs)
     units = [
@@ -413,6 +415,7 @@
         if n > 1:
             units[n - 2].last()
     params_ref[...] = small.collect(own_ref, R, D)
+    load.wait()
     lax.fori_loop(0, steps // 2, norm, 0)
     units[-1].relay()
     if at.M > 1:
@@ -433,14 +436,14 @@
     sems = (M, GatherUnit.count(G))
     return pl.pallas_call(
         functools.partial(entry_kernel, rows=min(256, L)),
-        in_specs=[VMEM] * 4,
+        in_specs=[ANY, VMEM, VMEM, VMEM],
         out_specs=[ANY, VMEM, VMEM],
         out_shape=[
             jax.ShapeDtypeStruct((3, G, 2, M, R, D), BF),
             jax.ShapeDtypeStruct((L, D), BF),
             jax.ShapeDtypeStruct((8, D), F32),
         ],
-        scratch_shapes=[pltpu.VMEM((3, R, D), BF), pltpu.VMEM((8, 128), F32), pltpu.VMEM((n, 8, 128), F32), DMA((M + 1,)), DMA((M,)), DMA(sems), DMA(sems), DMA((n,)), DMA((n,))],
+        scratch_shapes=[pltpu.VMEM((L, D), BF), DMA((1,)), pltpu.VMEM((3, R, D), BF), pltpu.VMEM((8, 128), F32), pltpu.VMEM((n, 8, 128), F32), DMA((M + 1,)), DMA((M,)), DMA(sems), DMA(sems), DMA((n,)), DMA((n,))],
         compiler_params=params_of(0),
     )(x, block, gain, bias)
 

time: 221 us -> 221 us (level)
  no operation moved by 1% of the time
where the time goes in v6:
time: 221 us; the launch traced here: 220 us
  Pallas kernels  211 us (95%)
  local copies, waits for them, and re-layouts  8.2 us (4%)
    pallas_call x1, Pallas kernels, attend_back(): pl.pallas_call(functools.partial(attend_back_kernel, tq=tq), grid=(pairs,...  63.4 us
    pallas_call x1, Pallas kernels, mlp(): pl.pallas_call(functools.partial(mlp_kernel, tr=tr), in_specs=[SMEM, ANY,...  48.1 us
    pallas_call x1, Pallas kernels, attend(): pl.pallas_call(functools.partial(attend_kernel, tq=tq), grid=(D // 128,),...  43.2 us
    pallas_call x1, Pallas kernels, entry(): pl.pallas_call(functools.partial(entry_kernel, rows=min(256, L)), in_spec...  34.6 us
    pallas_call x1, Pallas kernels, leave(): pl.pallas_call(functools.partial(exit_kernel, rows=min(256, L)), in_specs...  21.4 us
    unnamed x18, local copies, waits for them, and re-layouts  6.89 us

profile of v6, /device:TPU:0, one launch (start us, length us, event | category | flops | bytes accessed | tf_op | source)
XLA Modules:
  0.0 220.2 jit_solution(8560308956981614959)
XLA Ops:
  1.3 34.6 %shard_map.152 = (bf16[3,4,2,4,24,768]{5,4,3,2,1,0:T(8,128)(2,1)}, bf16[1024,768]{1,0:T(8,128)(2,1)}, f32[8,768]{1,0:T(8,128)}) custom-call(bf16[1024,768]{1,0:T(8,128)(2,1)} %x_hbm.5, bf16[24,2304]{1,0:T(8,128)(2,1)} %bitcast.32, bf16[2,24]{1,0:T(2,128)(2,1)} %bitcast.35, bf16[2,24]{1,0:T(2,128)(2,1)} %bitcast.36), custom_call_target="tpu_custom_call" | custom-call | tf_op jit(solution)/shard_map/pallas_call | solution.py:437
  35.8 43.2 %shard_map.153 = (bf16[1024,768]{1,0:T(8,128)(2,1)}, f32[1024,768]{1,0:T(8,128)}, f32[1024,128]{1,0:T(8,128)}, bf16[1024,2304]{1,0:T(8,128)(2,1)}, bf16[4,2,4,24...) custom-call(s32[1]{0:T(128)S(6)} %copy.23.len_ref, ...), custom_call_target="tpu_custom_call" | custom-call | tf_op jit(solution)/shard_map/pallas_call | solution.py:679
  79.1 48.1 %shard_map.154 = (bf16[1024,768]{1,0:T(8,128)(2,1)}, f32[1024,768]{1,0:T(8,128)}, bf16[1024,768]{1,0:T(8,128)(2,1)}, f32[8,768]{1,0:T(8,128)}, bf16[4,2,4,24,768...) custom-call(s32[1]{0:T(128)S(6)} %copy.23.len_ref, ...), custom_call_target="tpu_custom_call" | custom-call | tf_op jit(solution)/shard_map/pallas_call | solution.py:892
  127.2 63.4 %shard_map.155 = (bf16[3,1024,768]{2,1,0:T(8,128)(2,1)}, f32[96,768]{1,0:T(8,128)}, f32[96,768]{1,0:T(8,128)}, f32[24,768]{1,0:T(8,128)}, f32[2,24,768]{2,1,0:T(8,128)}, /*index=5*/bf16[4,2,4,24,768]{4,3,2,1,0:T(8,128)(2,1)}) custom-call(s32[1]{0:T(128)S(6)} %copy.23.len_ref, bf16[1024,2304]{1,0:T(8,128)(2,1)} %get-tuple-element.47.q_ref.k_ref.v_ref, ...), custom_call_target="tpu_custom_call" | custom-call | tf_op jit(solution)/shard_map/pallas_call | solution.py:1056
  190.6 0.0 copy-start.1
  190.6 21.4 %shard_map.156 = (f32[1024,768]{1,0:T(8,128)}, f32[24,2304]{1,0:T(8,128)}, f32[8,128]{1,0:T(8,128)}) custom-call(bf16[1024,768]{1,0:T(8,128)(2,1)} %x_hbm.5, bf16[3,1024,768]{2,1,0:T(8,128)(2,1)} %get-tuple-element.57.dqkv_hbm, bf16[3,768,768]{2,1,0:T(8,128)(2,1)} %bitcast.23, f32[1024,768]{1,0:T(8,128)} %get-tuple-element.58.mid_hbm, ...), custom_call_target="tpu_custom_call" | custom-call | tf_op jit(solution)/shard_map/pallas_call | solution.py:1173
  212.0 1.3 slice_bitcast_fusion
  213.3 0.0 copy-done.1
  213.3 0.0 copy-start
  213.3 1.1 copy.24
  214.4 1.3 copy-done
  215.8 0.0 copy-start.4
  215.8 0.0 copy-start.5
  215.8 0.0 copy-start.3
  215.8 0.0 copy-start.2
  215.8 1.7 copy.25
  217.4 0.0 copy-done.4
  217.4 0.7 copy.26
  218.1 0.0 copy-done.5
  218.1 0.6 copy.27
  218.8 0.0 copy-done.3
  218.8 0.7 copy.28
  219.5 0.0 copy-done.2
  219.5 0.7 copy.29
Async XLA Ops:
  190.6 22.7 %copy-start.1 = (bf16[1024,768]{1,0:T(8,128)(2,1)S(1)}, bf16[1024,768]{1,0:T(8,128)(2,1)}, u32[]{:S(2)}) copy-start(bf16[1024,768]{1,0:T(8,128)(2,1)} %get-tuple-element.78) | copy-start | bytes 4718596
  213.3 2.5 %copy-start = (f32[1024,768]{1,0:T(8,128)S(1)}, f32[1024,768]{1,0:T(8,128)}, u32[]{:S(2)}) copy-start(f32[1024,768]{1,0:T(8,128)} %get-tuple-element.79) | copy-start | bytes 9437188
  215.8 1.7 copy-start.4
  215.8 2.4 %copy-start.5 = (f32[24,768]{1,0:T(8,128)S(1)}, f32[24,768]{1,0:T(8,128)}, u32[]{:S(2)}) copy-start(f32[24,768]{1,0:T(8,128)} %get-tuple-element.64) | copy-start | bytes 221188
  215.8 3.0 %copy-start.3 = (f32[96,768]{1,0:T(8,128)S(1)}, f32[96,768]{1,0:T(8,128)}, u32[]{:S(2)}) copy-start(f32[96,768]{1,0:T(8,128)} %get-tuple-element.65) | copy-start | bytes 884740
  215.8 3.7 %copy-start.2 = (f32[96,768]{1,0:T(8,128)S(1)}, f32[96,768]{1,0:T(8,128)}, u32[]{:S(2)}) copy-start(f32[96,768]{1,0:T(8,128)} %get-tuple-element.66) | copy-start | bytes 884740
